TPU v7x, 32 devices: a whole 2x2x4 slice. The times are simulated.
32 devices in a mesh: dp: 2 (over core), context: 4 (over z), tensor: 4 (over y, x).
Axes of the slice: x: 2, y: 2, z: 4, core: 2. Of those that a mesh axis runs over, the one named last changes fastest.
Arguments:
- block_in: float32 [2, 2048, 1024], P('dp', 'context'), may hold values from -6 to 6
- segments: int32 [2, 2048], P('dp', 'context'), may hold values from 0 to 3, never falling along the last dimension, each value on 1 to 1024 neighbouring positions
- cotangent: float32 [2, 2048, 1024], P('dp', 'context'), may hold values from -6 to 6
- norm_gain: bfloat16 [1024], P(('dp', 'context')), may hold values from 0.5 to 1.5
- w_query: bfloat16 [1024, 512], P(('dp', 'context'), 'tensor'), may hold values from -0.1875 to 0.1875
- w_key: bfloat16 [1024, 512], P(('dp', 'context'), 'tensor'), may hold values from -0.1875 to 0.1875
- w_value: bfloat16 [1024, 1024], P(('dp', 'context'), 'tensor'), may hold values from -0.1875 to 0.1875
- w_gate_out: bfloat16 [1024, 1024], P(('dp', 'context'), 'tensor'), may hold values from -0.1875 to 0.1875
- w_rank_in: bfloat16 [1024, 16], P(('dp', 'context')), may hold values from -0.1875 to 0.1875
- w_rank_out: float32 [512, 16], P('tensor'), may hold values from -1.5 to 1.5
- gate_bias: float32 [512], P('tensor'), may hold values from 0 to 13
- group_gain: float32 [256], replicated, may hold values from 0.5 to 1.5
- w_output: bfloat16 [1024, 1024], P(('dp', 'context'), 'tensor'), may hold values from -0.25 to 0.25
- mlp_gain: bfloat16 [1024], P(('dp', 'context')), may hold values from 0.5 to 1.5
- w_gate: bfloat16 [1024, 2816], P(('dp', 'context'), 'tensor'), may hold values from -0.1875 to 0.1875
- w_up: bfloat16 [1024, 2816], P(('dp', 'context'), 'tensor'), may hold values from -0.1875 to 0.1875
- w_down: bfloat16 [1024, 2816], P(('dp', 'context'), 'tensor'), may hold values from -0.15625 to 0.15625
Outputs:
- block_out: float32 [2, 2048, 1024], P('dp', 'context')
- d_block_in: float32 [2, 2048, 1024], P('dp', 'context')
- d_norm_gain: float32 [1024], P(('dp', 'context'))
- d_w_query: float32 [1024, 512], P(('dp', 'context'), 'tensor')
- d_w_key: float32 [1024, 512], P(('dp', 'context'), 'tensor')
- d_w_value: float32 [1024, 1024], P(('dp', 'context'), 'tensor')
- d_w_gate_out: float32 [1024, 1024], P(('dp', 'context'), 'tensor')
- d_w_rank_in: float32 [1024, 16], P(('dp', 'context'))
- d_w_rank_out: float32 [512, 16], P('tensor')
- d_gate_bias: float32 [512], P('tensor')
- d_group_gain: float32 [256], replicated
- d_w_output: float32 [1024, 1024], P(('dp', 'context'), 'tensor')
- d_mlp_gain: float32 [1024], P(('dp', 'context'))
- d_w_gate: float32 [1024, 2816], P(('dp', 'context'), 'tensor')
- d_w_up: float32 [1024, 2816], P(('dp', 'context'), 'tensor')
- d_w_down: float32 [1024, 2816], P(('dp', 'context'), 'tensor')
Inputs may be any that keep to these rules, and one draw needn't show every extreme that they name: `segments`: along each sequence the segment numbers never fall; a document holds at most 1024 tokens and one holds exactly that many.
All inputs are finite; a program needn't handle non-finite values.
Results may differ from a plain program's by a relative error of at most 0.012.
Values may be sent and summed in bfloat16 or wider, within the bound.
A program may use at most 256 MiB of HBM per device.

v0:
```python
import jax
import jax.numpy as jnp
from jax import lax
from jax.sharding import PartitionSpec as P

HEAD_K = 128
HEAD_V = 256
BLOCK = 64


epsilon = 1e-06
gate_divisor = 16.0
highest_precision = lax.Precision.HIGHEST


def entering(shard, axis, combine, identity):
    peers, here = (lax.axis_size(axis), lax.axis_index(axis))
    everything = jax.tree.map(lambda part: lax.all_gather(part, axis), shard)
    start = jax.tree.map(
        lambda part, zero: jnp.broadcast_to(jnp.asarray(zero, part.dtype), part.shape),
        shard,
        identity,
    )

    def step(k, before):
        reached = k < here
        new = combine(before, jax.tree.map(lambda part: part[k], everything))
        return jax.tree.map(lambda a, b: jnp.where(reached, a, b), new, before)

    return lax.fori_loop(0, peers, step, start)


def entering_2(shard, axis, combine, identity):
    peers, here = (lax.axis_size(axis), lax.axis_index(axis))
    everything = jax.tree.map(
        lambda part, kind: lax.all_gather(part.astype(kind), axis),
        shard,
        jax.tree.map(lambda a: jnp.bfloat16 if a.dtype == jnp.float32 else a.dtype, shard),
    )
    start = jax.tree.map(
        lambda part, zero: jnp.broadcast_to(jnp.asarray(zero, part.dtype), part.shape),
        shard,
        identity,
    )

    def step(k, before):
        at = peers - 1 - k
        reached = at > here
        new = combine(
            before, jax.tree.map(lambda part, own: part[at].astype(own.dtype), everything, shard)
        )
        return jax.tree.map(lambda a, b: jnp.where(reached, a, b), new, before)

    return lax.fori_loop(0, peers, step, start)


def block_step(carried_in, pieces):
    carried_over, seg_prev = carried_in
    query_rows, key_vecs, value_vectors, decay_log, seg_block = pieces
    running_total = jnp.cumsum(decay_log, axis=0)
    length = query_rows.shape[0]
    causal = jnp.arange(length)[:, None] >= jnp.arange(length)[None, :]
    allowed = (causal & (seg_block[:, None] == seg_block[None, :]))[:, :, None, None]
    spread = running_total[:, None] - running_total[None, :]
    factor = jnp.where(allowed, jnp.exp(jnp.where(allowed, spread, 0.0)), 0.0)
    scores = jnp.einsum(
        "thk,shk,tshk->tsh", query_rows, key_vecs, factor, precision=highest_precision
    )
    output_rows = jnp.einsum("tsh,shv->thv", scores, value_vectors, precision=highest_precision)
    state_reading = (seg_block == seg_prev).astype(jnp.float32)[:, None, None]
    output_rows = output_rows + state_reading * jnp.einsum(
        "qou,ouj->qoj",
        query_rows * jnp.exp(running_total),
        carried_over,
        precision=highest_precision,
    )
    last_seg = seg_block[-1]
    in_tail = (seg_block == last_seg).astype(jnp.float32)[:, None, None]
    weighted_sum = key_vecs * jnp.exp(running_total[-1][None] - running_total) * in_tail
    keep_factor = (seg_prev == last_seg).astype(jnp.float32)
    carried_over = (
        jnp.einsum("mzp,mzx->zpx", weighted_sum, value_vectors, precision=highest_precision)
        + keep_factor * jnp.exp(running_total[-1])[:, :, None] * carried_over
    )
    return ((carried_over, last_seg), output_rows)


def local_core(query_rows, key_vecs, value_vectors, decay_log, seg_row):
    blocks = query_rows.shape[0] // BLOCK

    def to_blocks(values_in):
        return values_in.reshape((blocks, BLOCK) + values_in.shape[1:])

    initial = (
        jnp.zeros((query_rows.shape[1], query_rows.shape[2], value_vectors.shape[2]), jnp.float32),
        seg_row[0],
    )
    (state_end, _), output_rows = lax.scan(
        block_step,
        initial,
        (
            to_blocks(query_rows),
            to_blocks(key_vecs),
            to_blocks(value_vectors),
            to_blocks(decay_log),
            to_blocks(seg_row),
        ),
    )
    running_total = jnp.cumsum(decay_log, axis=0)
    unbroken = (seg_row[0] == seg_row[-1]).astype(jnp.float32)
    output_rows = output_rows.reshape(
        query_rows.shape[0], query_rows.shape[1], value_vectors.shape[2]
    )
    return (output_rows, state_end, jnp.exp(running_total[-1]) * unbroken, running_total)


def join_states(earlier, later):
    keep_factor = jnp.where(
        (later[2] == earlier[3]) | (earlier[3] < 0.0) | (later[2] < 0.0), 1.0, 0.0
    )
    passing = keep_factor * later[1]
    return (
        later[0] + passing[..., None] * earlier[0],
        passing * earlier[1],
        jnp.where(earlier[2] < 0.0, later[2], earlier[2]),
        jnp.where(later[3] < 0.0, earlier[3], later[3]),
    )


def join_grads(earlier, later):
    return (later[0] + later[1][..., None] * earlier[0], later[1] * earlier[1])


def gated_norm(mixed_core, out_gate, group_gain):
    inverse_rms = lax.rsqrt(jnp.mean(mixed_core * mixed_core, axis=-1, keepdims=True) + epsilon)
    return mixed_core * inverse_rms * group_gain * jax.nn.silu(out_gate)


def decay_map(rank_act, w_rank_out, gate_bias):
    return (
        jax.nn.log_sigmoid(jnp.dot(rank_act, w_rank_out.T, precision=highest_precision) + gate_bias)
        / gate_divisor
    )


def norm_back(scaled_grad, unit_rows, rstd_rows):
    return rstd_rows * (
        scaled_grad - unit_rows * jnp.mean(scaled_grad * unit_rows, axis=-1, keepdims=True)
    )


def project_back(grad_low, weight_full):
    return jnp.einsum("tk,dk->td", grad_low, weight_full, preferred_element_type=jnp.float32)


def weight_grad(normed_rows, grad_low):
    return jnp.einsum("td,tk->dk", normed_rows, grad_low, preferred_element_type=jnp.float32)


def per_device(
    block_in,
    segments,
    cotangent,
    norm_gain,
    w_query,
    w_key,
    w_value,
    w_gate_out,
    w_rank_in,
    w_rank_out,
    gate_bias,
    group_gain,
    w_output,
    mlp_gain,
    w_gate,
    w_up,
    w_down,
):
    hidden_in = block_in[0]
    seg_row = segments[0]
    grad_out = cotangent[0]
    tokens = hidden_in.shape[0]
    heads_here = w_rank_out.shape[0] // HEAD_K
    query_scale = HEAD_K ** (-0.5)
    attn_set = (
        lax.all_gather(norm_gain, ("dp", "context"), axis=0, tiled=True),
        lax.all_gather(w_query, ("dp", "context"), axis=0, tiled=True),
        lax.all_gather(w_key, ("dp", "context"), axis=0, tiled=True),
        lax.all_gather(w_value, ("dp", "context"), axis=0, tiled=True),
        lax.all_gather(w_gate_out, ("dp", "context"), axis=0, tiled=True),
        lax.all_gather(w_rank_in, ("dp", "context"), axis=0, tiled=True),
        lax.all_gather(w_output, ("dp", "context"), axis=0, tiled=True),
    )
    gain_one = attn_set[0].astype(jnp.float32)
    rstd_one = lax.rsqrt(jnp.mean(hidden_in * hidden_in, axis=-1, keepdims=True) + epsilon)
    unit_one = hidden_in * rstd_one
    normed_one = (unit_one * gain_one).astype(jnp.bfloat16)
    query_rows = jnp.dot(normed_one, attn_set[1], preferred_element_type=jnp.float32) * query_scale
    key_vecs = jnp.dot(normed_one, attn_set[2], preferred_element_type=jnp.float32)
    value_vectors = jnp.dot(normed_one, attn_set[3], preferred_element_type=jnp.float32)
    out_gate = jnp.dot(normed_one, attn_set[4], preferred_element_type=jnp.float32)
    rank_act = jnp.dot(normed_one, attn_set[5], preferred_element_type=jnp.float32)
    decay_log, decay_pull = jax.vjp(decay_map, rank_act, w_rank_out, gate_bias)
    query_heads = query_rows.reshape(tokens, heads_here, HEAD_K)
    key_heads = key_vecs.reshape(tokens, heads_here, HEAD_K)
    value_heads = value_vectors.reshape(tokens, heads_here, HEAD_V)
    decay_heads = decay_log.reshape(tokens, heads_here, HEAD_K)

    def local_part(query_part, key_part, value_part, decay_part):
        return local_core(query_part, key_part, value_part, decay_part, seg_row)

    (out_local, state_local, decay_span, running_total), local_pull = jax.vjp(
        local_part, query_heads, key_heads, value_heads, decay_heads
    )
    first_seg = seg_row[0].astype(jnp.float32)
    summary = (state_local, decay_span, first_seg, seg_row[-1].astype(jnp.float32))
    neutral = (
        jnp.zeros_like(state_local),
        jnp.ones_like(decay_span),
        jnp.float32(-1.0),
        jnp.float32(-1.0),
    )
    prior = entering(summary, "context", join_states, neutral)
    previous_state = prior[0]
    prior_last = prior[3]
    state_reading = (seg_row.astype(jnp.float32) == prior_last).astype(jnp.float32)[:, None, None]
    lifted_rows = query_heads * jnp.exp(running_total)
    mixed_core = out_local + state_reading * jnp.einsum(
        "qou,ouj->qoj", lifted_rows, previous_state, precision=highest_precision
    )
    gated_full, gate_pull = jax.vjp(
        gated_norm, mixed_core, out_gate.reshape(tokens, heads_here, HEAD_V), group_gain
    )
    gated_out = gated_full.reshape(tokens, heads_here * HEAD_V).astype(jnp.bfloat16)
    attn_part = jnp.einsum("tv,dv->td", gated_out, attn_set[6], preferred_element_type=jnp.float32)
    residual = hidden_in + lax.psum(attn_part, "tensor")
    mlp_set = (
        lax.all_gather(mlp_gain, ("dp", "context"), axis=0, tiled=True),
        lax.all_gather(w_gate, ("dp", "context"), axis=0, tiled=True),
        lax.all_gather(w_up, ("dp", "context"), axis=0, tiled=True),
        lax.all_gather(w_down, ("dp", "context"), axis=0, tiled=True),
    )
    gain_two = mlp_set[0].astype(jnp.float32)
    rstd_two = lax.rsqrt(jnp.mean(residual * residual, axis=-1, keepdims=True) + epsilon)
    unit_two = residual * rstd_two
    normed_two = (unit_two * gain_two).astype(jnp.bfloat16)
    gate_pre = jnp.dot(normed_two, mlp_set[1], preferred_element_type=jnp.float32)
    up_value = jnp.dot(normed_two, mlp_set[2], preferred_element_type=jnp.float32)
    sigmoid_gate = jax.nn.sigmoid(gate_pre)
    activation = (gate_pre * sigmoid_gate * up_value).astype(jnp.bfloat16)
    mlp_part = jnp.einsum("tf,df->td", activation, mlp_set[3], preferred_element_type=jnp.float32)
    block_out = residual + lax.psum(mlp_part.astype(jnp.bfloat16), "tensor").astype(jnp.float32)
    grad_low = grad_out.astype(jnp.bfloat16)
    d_activation = jnp.dot(grad_low, mlp_set[3], preferred_element_type=jnp.float32)
    d_w_down = weight_grad(grad_low, activation)
    d_gate_pre = (
        d_activation * up_value * sigmoid_gate * (1.0 + gate_pre * (1.0 - sigmoid_gate))
    ).astype(jnp.bfloat16)
    d_up_value = (d_activation * gate_pre * sigmoid_gate).astype(jnp.bfloat16)
    d_w_gate = weight_grad(normed_two, d_gate_pre)
    d_w_up = weight_grad(normed_two, d_up_value)
    dnormed_part = project_back(d_gate_pre, mlp_set[1]) + project_back(d_up_value, mlp_set[2])
    dnormed_two = lax.psum(dnormed_part, "tensor")
    gain_local = jnp.sum(dnormed_two * unit_two, axis=0)
    gain_shared = jnp.zeros_like(gain_local)
    d_residual = grad_out + norm_back(dnormed_two * gain_two, unit_two, rstd_two)
    residual_low = d_residual.astype(jnp.bfloat16)
    d_gated_out = jnp.dot(residual_low, attn_set[6], preferred_element_type=jnp.float32)
    d_w_output = weight_grad(residual_low, gated_out)
    mixed_core_gradient, d_out_gate, gain_part = gate_pull(
        d_gated_out.reshape(tokens, heads_here, HEAD_V)
    )
    direct_term = jnp.einsum(
        "jeu,jel->eul",
        state_reading * lifted_rows,
        mixed_core_gradient,
        precision=highest_precision,
    )
    open_flag = jnp.where((prior_last == first_seg) | (prior_last < 0.0), 1.0, 0.0)
    passing = decay_span * open_flag
    later = entering_2(
        (direct_term, passing),
        "context",
        join_grads,
        (jnp.zeros_like(direct_term), jnp.ones_like(passing)),
    )
    later_grad = later[0]
    d_decay_span = open_flag * jnp.sum(previous_state * later_grad, axis=-1)
    pulled_back = (
        jnp.einsum("mna,nwa->mnw", mixed_core_gradient, previous_state, precision=highest_precision)
        * state_reading
    )
    d_cumulative = pulled_back * lifted_rows
    d_query_heads, d_key_heads, d_value_heads, d_decay_heads = local_pull(
        (mixed_core_gradient, later_grad, d_decay_span, d_cumulative)
    )
    d_query_heads = d_query_heads + pulled_back * jnp.exp(running_total)
    rank_part, d_w_rank_out_part, d_bias_part = decay_pull(
        d_decay_heads.reshape(tokens, heads_here * HEAD_K)
    )
    query_low = (d_query_heads.reshape(tokens, heads_here * HEAD_K) * query_scale).astype(
        jnp.bfloat16
    )
    key_low = d_key_heads.reshape(tokens, heads_here * HEAD_K).astype(jnp.bfloat16)
    value_low = d_value_heads.reshape(tokens, heads_here * HEAD_V).astype(jnp.bfloat16)
    gate_low = d_out_gate.reshape(tokens, heads_here * HEAD_V).astype(jnp.bfloat16)
    dnormed_part = (
        project_back(query_low, attn_set[1])
        + project_back(key_low, attn_set[2])
        + project_back(value_low, attn_set[3])
        + project_back(gate_low, attn_set[4])
    )
    summed = lax.psum((dnormed_part, rank_part, gain_part, gain_shared), "tensor")
    d_mlp_gain = gain_local + summed[3]
    mlp_grads = (
        lax.psum_scatter(d_mlp_gain, ("dp", "context"), scatter_dimension=0, tiled=True),
        lax.psum_scatter(d_w_gate, ("dp", "context"), scatter_dimension=0, tiled=True),
        lax.psum_scatter(d_w_up, ("dp", "context"), scatter_dimension=0, tiled=True),
        lax.psum_scatter(d_w_down, ("dp", "context"), scatter_dimension=0, tiled=True),
    )
    rank_low = summed[1].astype(jnp.bfloat16)
    dnormed_one = summed[0] + project_back(rank_low, attn_set[5])
    d_w_query = weight_grad(normed_one, query_low)
    d_w_key = weight_grad(normed_one, key_low)
    d_w_value = weight_grad(normed_one, value_low)
    d_w_gate_out = weight_grad(normed_one, gate_low)
    d_w_rank_in = weight_grad(normed_one, rank_low)
    d_norm_gain = jnp.sum(dnormed_one * unit_one, axis=0)
    d_block_in = d_residual + norm_back(dnormed_one * gain_one, unit_one, rstd_one)
    attn_grads = (
        lax.psum_scatter(d_norm_gain, ("dp", "context"), scatter_dimension=0, tiled=True),
        lax.psum_scatter(d_w_query, ("dp", "context"), scatter_dimension=0, tiled=True),
        lax.psum_scatter(d_w_key, ("dp", "context"), scatter_dimension=0, tiled=True),
        lax.psum_scatter(d_w_value, ("dp", "context"), scatter_dimension=0, tiled=True),
        lax.psum_scatter(d_w_gate_out, ("dp", "context"), scatter_dimension=0, tiled=True),
        lax.psum_scatter(d_w_rank_in, ("dp", "context"), scatter_dimension=0, tiled=True),
        lax.psum_scatter(d_w_output, ("dp", "context"), scatter_dimension=0, tiled=True),
    )
    small = lax.psum((d_w_rank_out_part, d_bias_part, summed[2]), ("dp", "context"))
    return (
        block_out[None],
        d_block_in[None],
        attn_grads[0],
        attn_grads[1],
        attn_grads[2],
        attn_grads[3],
        attn_grads[4],
        attn_grads[5],
        small[0],
        small[1],
        small[2],
        attn_grads[6],
        mlp_grads[0],
        mlp_grads[1],
        mlp_grads[2],
        mlp_grads[3],
    )


def solution(mesh):
    placed = (
        P("dp", "context", None),
        P("dp", "context"),
        P("dp", "context", None),
        P(("dp", "context")),
        P(("dp", "context"), "tensor"),
        P(("dp", "context"), "tensor"),
        P(("dp", "context"), "tensor"),
        P(("dp", "context"), "tensor"),
        P(("dp", "context"), None),
        P("tensor", None),
        P("tensor"),
        P(),
        P(("dp", "context"), "tensor"),
        P(("dp", "context")),
        P(("dp", "context"), "tensor"),
        P(("dp", "context"), "tensor"),
        P(("dp", "context"), "tensor"),
    )
    return jax.shard_map(
        per_device,
        mesh=mesh,
        in_specs=placed,
        out_specs=(
            P("dp", "context", None),
            P("dp", "context", None),
            P(("dp", "context")),
            P(("dp", "context"), "tensor"),
            P(("dp", "context"), "tensor"),
            P(("dp", "context"), "tensor"),
            P(("dp", "context"), "tensor"),
            P(("dp", "context"), None),
            P("tensor", None),
            P("tensor"),
            P(),
            P(("dp", "context"), "tensor"),
            P(("dp", "context")),
            P(("dp", "context"), "tensor"),
            P(("dp", "context"), "tensor"),
            P(("dp", "context"), "tensor"),
        ),
        check_vma=False,
    )
```

profile of v0, /device:TPU:0, one launch (start us, length us, event | category | flops | bytes accessed | tf_op | source)
XLA Modules:
  0.0 1442.9 jit_solution(13011966884912869483)
XLA Ops:
  8.1 17.5 %all-gather.2 = bf16[8,1,128]{2,1,0:T(2,128)(2,1)S(1)} all-gather(bf16[1,1,128]{2,1,0:T(2,128)(2,1)} %bitcast.929), channel_id=1, replica_groups=mesh['dp'=2,'context'=4,'tensor'=4] {'dp','context'}, dimensions={0}, use_global_device_ids=true | all-gather | bytes 2304 | tf_op jit(solution)/shard_map/all_gather | solution.py:186
  29.1 21.1 %all_gather.67 = bf16[1024,16]{0,1:T(8,128)(2,1)S(1)} all-gather(bf16[128,16]{0,1:T(8,128)(2,1)S(1)} %copy-done.67), channel_id=1, replica_groups=mesh['dp'=2,'context'=4,'tensor'=4] {'dp','context'}, dimensions={0}, use_global_device_ids=true | all-gather | bytes 36864 | tf_op jit(solution)/shard_map/all_gather | solution.py:191
  57.8 26.1 %all_gather.68 = bf16[1024,256]{1,0:T(8,128)(2,1)S(1)} all-gather(bf16[128,256]{1,0:T(8,128)(2,1)S(1)} %copy-done.52), channel_id=1, replica_groups=mesh['dp'=2,'context'=4,'tensor'=4] {'dp','context'}, dimensions={0}, use_global_device_ids=true | all-gather | bytes 589824 | tf_op jit(solution)/shard_map/all_gather | solution.py:189
  86.5 25.3 %all_gather.66 = bf16[1024,128]{1,0:T(8,128)(2,1)S(1)} all-gather(bf16[128,128]{1,0:T(8,128)(2,1)S(1)} %copy-done.58), channel_id=1, replica_groups=mesh['dp'=2,'context'=4,'tensor'=4] {'dp','context'}, dimensions={0}, use_global_device_ids=true | all-gather | bytes 294912 | tf_op jit(solution)/shard_map/all_gather | solution.py:188
  113.7 25.2 %all_gather.69 = bf16[1024,128]{1,0:T(8,128)(2,1)S(1)} all-gather(bf16[128,128]{1,0:T(8,128)(2,1)S(1)} %copy-done.59), channel_id=1, replica_groups=mesh['dp'=2,'context'=4,'tensor'=4] {'dp','context'}, dimensions={0}, use_global_device_ids=true | all-gather | bytes 294912 | tf_op jit(solution)/shard_map/all_gather | solution.py:187
  144.9 283.5 %while.109 = (s32[]{:T(128)}, f32[1,128,256]{2,1,0:T(8,128)S(1)}, s32[]{:T(128)}, f32[8,64,1,256]{3,1,2,0:T(8,128)}, pred[8,64,64,1,128]{4,2,1,3,0:T(8,128)(4,1)...) while((s32[]{:T(128)}, f32[1,128,256]{2,1,0:T(8,128)S(1)}, ...), condition=%wide.region_3.4_spmd.clone.clone, body=%wide.region_1.3_spmd.clone.sunk.clone | while | flops 68944640 | bytes 27835304 | solution.py:98
  170.8 6.9 fusion.335
  206.2 6.8 fusion.335
  241.7 6.8 fusion.335
  277.1 6.8 fusion.335
  312.6 6.8 fusion.335
  348.1 6.8 fusion.335
  383.5 6.8 fusion.335
  418.9 6.9 fusion.335
  428.4 16.0 %all-gather = f32[4,128,256]{2,1,0:T(8,128)S(1)} all-gather(f32[1,128,256]{2,1,0:T(8,128)S(1)} %get-tuple-element.1180), channel_id=2, replica_groups=mesh['dp'=2,'context'=4,'tensor'=4] {'context'}, dimensions={0}, use_global_device_ids=true | all-gather | bytes 655360 | tf_op jit(solution)/shard_map/all_gather | solution.py:18
  446.3 8.7 all_gather.74
  457.8 9.2 all-reduce.9
  467.0 15.7 %while.110 = (s32[]{:T(128)}, f32[1,128,256]{2,1,0:T(8,128)S(1)}, f32[]{:T(128)}, s32[]{:T(128)}, f32[4,1,128,256]{3,2,1,0:T(8,128)S(1)}, /*index=5*/f32[4]{0:T(128)S(1)}, f32[4,1,128]{2,1,0:T(1,128)S(1)}, f32[4]{0:T(128)S(1)}) while((s32[]{:T(128)}, f32[1,128,256]{2,1,0:T(8,128)S(1)}, f32[]{:T(128)}, s32[]{:T(128)}, ...), condition=%wide.region_7.8_spmd.clone.clone, body=%wide.region_6.7_spmd.clone.sunk.clone | while | flops 131213 | bytes 394974 | solution.py:30
  486.9 25.2 %all_gather.77 = bf16[1024,256]{1,0:T(8,128)(2,1)S(1)} all-gather(bf16[128,256]{1,0:T(8,128)(2,1)S(1)} %copy-done.53), channel_id=1, replica_groups=mesh['dp'=2,'context'=4,'tensor'=4] {'dp','context'}, dimensions={0}, use_global_device_ids=true | all-gather | bytes 589824 | tf_op jit(solution)/shard_map/all_gather | solution.py:190
  512.6 26.1 %all_gather.78 = bf16[1024,256]{1,0:T(8,128)(2,1)S(1)} all-gather(bf16[128,256]{1,0:T(8,128)(2,1)S(1)} %copy-done.54), channel_id=1, replica_groups=mesh['dp'=2,'context'=4,'tensor'=4] {'dp','context'}, dimensions={0}, use_global_device_ids=true | all-gather | bytes 589824 | tf_op jit(solution)/shard_map/all_gather | solution.py:192
  543.9 16.6 %all-gather.3 = bf16[8,1,128]{2,1,0:T(2,128)(2,1)S(1)} all-gather(bf16[1,1,128]{2,1,0:T(2,128)(2,1)S(1)} %bitcast.930), channel_id=1, replica_groups=mesh['dp'=2,'context'=4,'tensor'=4] {'dp','context'}, dimensions={0}, use_global_device_ids=true | all-gather | bytes 2304 | tf_op jit(solution)/shard_map/all_gather | solution.py:238
  560.5 52.6 %all-reduce.15.cloned.1.call-done = f32[512,1024]{1,0:T(8,128)} async-done(((f32[512,1024]{1,0:T(8,128)}), f32[512,1024]{1,0:T(8,128)}) %all-reduce.15.cloned.1.call-update) | async-done | bytes 2097168 | tf_op jit(solution)/shard_map/psum | solution.py:236
  619.2 3.8 fusion.156
  623.0 3.8 fusion.157
  626.8 5.3 multiply_convert_fusion.3
  636.4 3.6 convolution_convert_fusion
  642.2 10.9 all_gather.85
  654.4 51.4 %all-reduce.19.cloned.1.call-done = f32[512,1024]{1,0:T(8,128)} async-done(((f32[512,1024]{1,0:T(8,128)}), f32[512,1024]{1,0:T(8,128)}) %all-reduce.19.cloned.1.call-update) | async-done | bytes 2097168 | tf_op jit(solution)/shard_map/psum | solution.py:263
  709.3 52.1 %all-reduce.17.cloned.1.call-done = bf16[512,1024]{1,0:T(8,128)(2,1)} async-done(((bf16[512,1024]{1,0:T(8,128)(2,1)}), bf16[512,1024]{1,0:T(8,128)(2,1)}) %all-reduce.17.cloned.1.call-update) | async-done | bytes 1048592 | tf_op jit(solution)/shard_map/psum | solution.py:252
  761.4 5.1 bitcast_add_fusion.6
  771.3 14.8 %all-gather.1 = bf16[512,256]{1,0:T(8,128)(2,1)} all-gather(bf16[128,256]{1,0:T(8,128)(2,1)S(1)} %convolution_convert_fusion.1), channel_id=3, replica_groups=mesh['dp'=2,'context'=4,'tensor'=4] {'context'}, dimensions={0}, use_global_device_ids=true | all-gather | bytes 327680 | tf_op jit(solution)/shard_map/all_gather | solution.py:36
  786.2 3.9 while.111
  793.1 199.9 %while.108 = (s32[]{:T(128)}, f32[1,128,256]{1,2,0:T(8,128)S(1)}, f32[8,64,1,128]{3,1,2,0:T(8,128)}, bf16[8,64,1,128]{3,1,2,0:T(8,128)(2,1)}, bf16[8,64,1,256]{3...) while((s32[]{:T(128)}, f32[1,128,256]{1,2,0:T(8,128)S(1)}, ...), condition=%wide.region_23.24_spmd.clone, body=%wide.region_17.23_spmd.sunk.clone | while | flops 132923392 | bytes 17227604 | solution.py:98
  1003.7 18.6 %all-reduce.8 = (bf16[512,16]{0,1:T(8,128)(2,1)}, f32[256]{0:T(256)S(1)}) all-reduce(f32[512,16]{0,1:T(8,128)} %fusion.131, f32[256]{0:T(256)S(1)} %copy-done.70), channel_id=1, replica_groups=mesh['dp'=2,'context'=4,'tensor'=4] {'tensor'}, use_global_device_ids=true, to_apply=%region_28.29 | all-reduce | flops 8448 | bytes 51200 | tf_op jit(solution)/shard_map/psum | solution.py:313
  1036.3 3.9 fusion.163
  1041.5 3.6 fusion.162
  1046.3 4.1 convolution_bitcast_fusion.6
  1052.6 17.6 %all-reduce.21.cloned.1.call-done = f32[512,1024]{1,0:T(8,128)} async-done(((f32[512,1024]{1,0:T(8,128)}), f32[512,1024]{1,0:T(8,128)}) %all-reduce.21.cloned.1.call-update) | async-done | bytes 2097168 | tf_op jit(solution)/shard_map/psum | solution.py:313
  1070.3 3.8 multiply_reduce_fusion.1
  1074.0 29.8 %all-reduce.7 = (f32[1024]{0:T(1024)S(1)}, f32[128,16]{0,1:T(8,128)}, f32[128]{0:T(128)}, f32[256]{0:T(256)}, f32[1024]{0:T(1024)S(1)}) all-reduce(f32[1024]{0:T(1024)S(1)} %get-tuple-element.1515, f32[128,16]{0,1:T(8,128)S(1)} %fusion.129, f32[128]{0:T(128)S(1)} %neg.57, ...), channel_id=4, replica_groups=mesh['dp'=2,'context'=4,'tensor'=4] {'dp','context'}, use_global_device_ids=true, to_apply=%region_31.32.clone | all-reduce | flops 4480 | bytes 35840
  1105.0 4.1 add_bitcast_fusion
  1109.1 16.1 %reduce-scatter.12.cloned.1.call-done = f32[128,128]{1,0:T(8,128)} async-done(((f32[1024,128]{1,0:T(8,128)}), f32[128,128]{1,0:T(8,128)}) %reduce-scatter.12.cloned.1.call-update) | async-done | bytes 65552 | tf_op jit(solution)/shard_map/reduce_scatter | solution.py:333
  1125.3 37.1 %reduce-scatter.20.cloned.1.call-done = f32[128,256]{1,0:T(8,128)} async-done(((f32[1024,256]{1,0:T(8,128)}), f32[128,256]{1,0:T(8,128)}) %reduce-scatter.20.cloned.1.call-update) | async-done | bytes 131088 | tf_op jit(solution)/shard_map/reduce_scatter | solution.py:337
  1162.4 37.7 %reduce-scatter.14.cloned.1.call-done = f32[128,256]{1,0:T(8,128)} async-done(((f32[1024,256]{1,0:T(8,128)}), f32[128,256]{1,0:T(8,128)}) %reduce-scatter.14.cloned.1.call-update) | async-done | bytes 131088 | tf_op jit(solution)/shard_map/reduce_scatter | solution.py:334
  1200.1 37.8 %reduce-scatter.16.cloned.1.call-done = f32[128,256]{1,0:T(8,128)} async-done(((f32[1024,256]{1,0:T(8,128)}), f32[128,256]{1,0:T(8,128)}) %reduce-scatter.16.cloned.1.call-update) | async-done | bytes 131088 | tf_op jit(solution)/shard_map/reduce_scatter | solution.py:335
  1237.9 65.7 %reduce-scatter.24.cloned.1.call-done = f32[128,704]{0,1:T(8,128)} async-done(((f32[1024,704]{0,1:T(8,128)}), f32[128,704]{0,1:T(8,128)}) %reduce-scatter.24.cloned.1.call-update) | async-done | bytes 360464 | tf_op jit(solution)/shard_map/reduce_scatter | solution.py:318
  1303.6 65.8 %reduce-scatter.22.cloned.1.call-done = f32[128,704]{0,1:T(8,128)} async-done(((f32[1024,704]{0,1:T(8,128)}), f32[128,704]{0,1:T(8,128)}) %reduce-scatter.22.cloned.1.call-update) | async-done | bytes 360464 | tf_op jit(solution)/shard_map/reduce_scatter | solution.py:317
  1369.4 65.9 %reduce-scatter.26.cloned.1.call-done = f32[128,704]{0,1:T(8,128)} async-done(((f32[1024,704]{0,1:T(8,128)}), f32[128,704]{0,1:T(8,128)}) %reduce-scatter.26.cloned.1.call-update) | async-done | bytes 360464 | tf_op jit(solution)/shard_map/reduce_scatter | solution.py:319
  (971 shorter events, 512.6 us)
Async XLA Ops:
  8.0 43.8 %copy-start = (f32[128,16]{0,1:T(8,128)S(1)}, f32[128,16]{0,1:T(8,128)}, u32[]{:S(2)}) copy-start(f32[128,16]{0,1:T(8,128)} %param.34) | copy-start | bytes 24580
  8.0 19.4 %copy-start.1 = (f32[1,512,1024]{2,1,0:T(8,128)S(1)}, f32[1,512,1024]{2,1,0:T(8,128)}, u32[]{:S(2)}) copy-start(f32[1,512,1024]{2,1,0:T(8,128)} %param.25) | copy-start | bytes 6291460
  8.0 605.0 %all-reduce.15.cloned.1.call-start = ((), (), s32[]{:S(2)}) async-start(), calls=%async_computation.9 | async-start | bytes 4194304 | tf_op jit(solution)/shard_map/psum | solution.py:236
  27.7 24.0 %copy-start.75 = (f32[128]{0:T(128)S(1)}, f32[128]{0:T(128)}, u32[]{:S(2)}) copy-start(f32[128]{0:T(128)} %param.35) | copy-start | bytes 1540
  29.0 25.7 %copy-start.63 = (s32[1,512]{1,0:T(1,128)S(1)}, s32[1,512]{1,0:T(1,128)}, u32[]{:S(2)}) copy-start(s32[1,512]{1,0:T(1,128)} %param.26) | copy-start | bytes 6148
  29.0 28.9 %copy-start.52 = (bf16[128,256]{1,0:T(8,128)(2,1)S(1)}, bf16[128,256]{1,0:T(8,128)(2,1)}, u32[]{:S(2)}) copy-start(bf16[128,256]{1,0:T(8,128)(2,1)} %param.31) | copy-start | bytes 196612
  51.8 33.4 %copy-start.43 = (f32[512,16]{0,1:T(8,128)}, f32[512,16]{0,1:T(8,128)S(1)}, u32[]{:S(2)}) copy-start(f32[512,16]{0,1:T(8,128)S(1)} %fusion.153) | copy-start | bytes 98308
  53.9 32.6 %copy-start.58 = (bf16[128,128]{1,0:T(8,128)(2,1)S(1)}, bf16[128,128]{1,0:T(8,128)(2,1)}, u32[]{:S(2)}) copy-start(bf16[128,128]{1,0:T(8,128)(2,1)} %param.30) | copy-start | bytes 98308
  84.7 29.0 %copy-start.59 = (bf16[128,128]{1,0:T(8,128)(2,1)S(1)}, bf16[128,128]{1,0:T(8,128)(2,1)}, u32[]{:S(2)}) copy-start(bf16[128,128]{1,0:T(8,128)(2,1)} %param.29) | copy-start | bytes 98308
  85.2 54.4 %copy-start.3 = (bf16[512,1024]{1,0:T(8,128)(2,1)S(1)}, bf16[512,1024]{1,0:T(8,128)(2,1)}, u32[]{:S(2)}) copy-start(bf16[512,1024]{1,0:T(8,128)(2,1)} %multiply_convert_fusion.1) | copy-start | bytes 3145732
  170.8 9.5 copy-start.66
  277.1 9.5 copy-start.36
  277.1 9.5 copy-start.66
  428.4 54.3 %copy-start.64 = (s32[1,512]{1,0:T(1,128)S(1)}, s32[1,512]{1,0:T(1,128)}, u32[]{:S(2)}) copy-start(s32[1,512]{1,0:T(1,128)} %param.26) | copy-start | bytes 6148
  445.2 39.7 %copy-start.19 = (f32[128,4,128]{0,2,1:T(8,128)}, f32[128,4,128]{0,2,1:T(8,128)S(1)}, u32[]{:S(2)}) copy-start(f32[128,4,128]{0,2,1:T(8,128)S(1)} %broadcast.602) | copy-start | bytes 786436
  445.2 39.7 %copy-start.9 = (f32[8,64,1,128]{3,1,2,0:T(8,128)S(1)}, f32[8,64,1,128]{3,1,2,0:T(8,128)}, u32[]{:S(2)}) copy-start(f32[8,64,1,128]{3,1,2,0:T(8,128)} %get-tuple-element.2505) | copy-start | bytes 786436
  445.2 39.7 %copy-start.18 = (f32[128,1,4,128]{0,3,2,1:T(8,128)S(1)}, f32[128,1,4,128]{0,3,2,1:T(8,128)}, u32[]{:S(2)}) copy-start(f32[128,1,4,128]{0,3,2,1:T(8,128)} %copy.114) | copy-start | bytes 786436
  446.3 38.6 %copy-start.42 = (f32[512,1,128]{2,0,1:T(8,128)}, f32[512,1,128]{2,0,1:T(8,128)S(1)}, u32[]{:S(2)}) copy-start(f32[512,1,128]{2,0,1:T(8,128)S(1)} %fusion.122) | copy-start | bytes 786436
  482.7 29.4 %copy-start.4 = (bf16[512,1024]{1,0:T(8,128)(2,1)S(1)}, bf16[512,1024]{1,0:T(8,128)(2,1)}, u32[]{:S(2)}) copy-start(bf16[512,1024]{1,0:T(8,128)(2,1)} %multiply_convert_fusion.1) | copy-start | bytes 3145732
  484.9 27.7 %copy-start.54 = (bf16[128,256]{1,0:T(8,128)(2,1)S(1)}, bf16[128,256]{1,0:T(8,128)(2,1)}, u32[]{:S(2)}) copy-start(bf16[128,256]{1,0:T(8,128)(2,1)} %param.37) | copy-start | bytes 196612
  485.0 53.8 %copy-start.68 = (f32[256]{0:T(256)S(1)}, f32[256]{0:T(256)}, u32[]{:S(2)}) copy-start(f32[256]{0:T(256)} %param.36) | copy-start | bytes 3076
  486.8 51.9 %copy-start.14 = (f32[512,1,256]{0,2,1:T(8,128)}, f32[512,1,256]{0,2,1:T(8,128)S(1)}, u32[]{:S(2)}) copy-start(f32[512,1,256]{0,2,1:T(8,128)S(1)} %get-tuple-element.1695) | copy-start | bytes 1572868
  486.9 52.1 %copy-start.60 = (f32[512]{0:T(512)}, f32[512]{0:T(512)S(1)}, u32[]{:S(2)}) copy-start(f32[512]{0:T(512)S(1)} %fusion.141) | copy-start | bytes 6148
  512.1 26.6 %copy-start.10 = (bf16[1024,256]{1,0:T(8,128)(2,1)}, bf16[1024,256]{1,0:T(8,128)(2,1)S(1)}, u32[]{:S(2)}) copy-start(bf16[1024,256]{1,0:T(8,128)(2,1)S(1)} %all_gather.77) | copy-start | bytes 1572868
  512.6 26.4 %copy-start.16 = (f32[512,256]{0,1:T(8,128)}, f32[512,256]{0,1:T(8,128)S(1)}, u32[]{:S(2)}) copy-start(f32[512,256]{0,1:T(8,128)S(1)} %fusion.154) | copy-start | bytes 1572868
  540.3 72.8 %copy-start.2 = (f32[1,512,1024]{2,1,0:T(8,128)S(1)}, f32[1,512,1024]{2,1,0:T(8,128)}, u32[]{:S(2)}) copy-start(f32[1,512,1024]{2,1,0:T(8,128)} %param.25) | copy-start | bytes 6291460
  542.1 77.1 %all-gather.8.cloned.1.call-start = ((), (), s32[]{:S(2)}) async-start(), calls=%async_computation.10 | async-start | bytes 1622016 | tf_op jit(solution)/shard_map/all_gather | solution.py:239
  542.7 80.3 %all-gather.10.cloned.1.call-start = ((), (), s32[]{:S(2)}) async-start(), calls=%async_computation.11 | async-start | bytes 1622016 | tf_op jit(solution)/shard_map/all_gather | solution.py:240
  543.3 83.5 %all-gather.12.cloned.1.call-start = ((), (), s32[]{:S(2)}) async-start(), calls=%async_computation.12 | async-start | bytes 1622016 | tf_op jit(solution)/shard_map/all_gather | solution.py:241
  543.8 162.0 %all-reduce.19.cloned.1.call-start = ((), (), s32[]{:S(2)}) async-start(), calls=%async_computation.14 | async-start | bytes 4194304 | tf_op jit(solution)/shard_map/psum | solution.py:263
  636.3 125.1 %all-reduce.17.cloned.1.call-start = ((), (), s32[]{:S(2)}) async-start(), calls=%async_computation.13 | async-start | bytes 2097152 | tf_op jit(solution)/shard_map/psum | solution.py:252
  640.0 430.3 %all-reduce.21.cloned.1.call-start = ((), (), s32[]{:S(2)}) async-start(), calls=%async_computation.15 | async-start | bytes 4194304 | tf_op jit(solution)/shard_map/psum | solution.py:313
  709.3 57.3 %copy-start.61 = (f32[512]{0:T(512)S(1)}, f32[512]{0:T(512)}, u32[]{:S(2)}) copy-start(f32[512]{0:T(512)} %copy-done.60) | copy-start | bytes 6148
  709.3 57.3 %copy-start.69 = (f32[256]{0:T(256)S(1)}, f32[256]{0:T(256)}, u32[]{:S(2)}) copy-start(f32[256]{0:T(256)} %param.36) | copy-start | bytes 3076
  998.9 110.3 %reduce-scatter.18.cloned.1.call-start = ((), (), s32[]{:S(2)}) async-start(), calls=%async_computation.20 | async-start | bytes 73728 | tf_op jit(solution)/shard_map/reduce_scatter | solution.py:336
  1024.5 84.7 %reduce-scatter.10.cloned.1.call-start = ((), (), s32[]{:S(2)}) async-start(), calls=%async_computation.16 | async-start | bytes 589824 | tf_op jit(solution)/shard_map/reduce_scatter | solution.py:332
  1025.8 99.4 %reduce-scatter.12.cloned.1.call-start = ((), (), s32[]{:S(2)}) async-start(), calls=%async_computation.17 | async-start | bytes 589824 | tf_op jit(solution)/shard_map/reduce_scatter | solution.py:333
  1028.1 134.3 %reduce-scatter.20.cloned.1.call-start = ((), (), s32[]{:S(2)}) async-start(), calls=%async_computation.21 | async-start | bytes 1179648 | tf_op jit(solution)/shard_map/reduce_scatter | solution.py:337
  1031.3 168.9 %reduce-scatter.14.cloned.1.call-start = ((), (), s32[]{:S(2)}) async-start(), calls=%async_computation.18 | async-start | bytes 1179648 | tf_op jit(solution)/shard_map/reduce_scatter | solution.py:334
  1033.7 204.1 %reduce-scatter.16.cloned.1.call-start = ((), (), s32[]{:S(2)}) async-start(), calls=%async_computation.19 | async-start | bytes 1179648 | tf_op jit(solution)/shard_map/reduce_scatter | solution.py:335
  1036.3 267.3 %reduce-scatter.24.cloned.1.call-start = ((), (), s32[]{:S(2)}) async-start(), calls=%async_computation.23 | async-start | bytes 3244032 | tf_op jit(solution)/shard_map/reduce_scatter | solution.py:318
  1040.3 329.1 %reduce-scatter.22.cloned.1.call-start = ((), (), s32[]{:S(2)}) async-start(), calls=%async_computation.22 | async-start | bytes 3244032 | tf_op jit(solution)/shard_map/reduce_scatter | solution.py:317
  1045.2 390.1 %reduce-scatter.26.cloned.1.call-start = ((), (), s32[]{:S(2)}) async-start(), calls=%async_computation.24 | async-start | bytes 3244032 | tf_op jit(solution)/shard_map/reduce_scatter | solution.py:319
  1050.4 19.8 %copy-start.41 = (bf16[1024,16]{0,1:T(8,128)(2,1)S(1)}, bf16[1024,16]{0,1:T(8,128)(2,1)}, u32[]{:S(2)}) copy-start(bf16[1024,16]{0,1:T(8,128)(2,1)} %copy-done.40) | copy-start | bytes 98308
  1050.4 19.8 %copy-start.50 = (f32[8,1,128]{2,1,0:T(1,128)S(1)}, f32[8,1,128]{2,1,0:T(1,128)}, u32[]{:S(2)}) copy-start(f32[8,1,128]{2,1,0:T(1,128)} %copy-done.49) | copy-start | bytes 12292
  1050.4 19.8 %copy-start.51 = (bf16[512,16]{0,1:T(8,128)(2,1)S(1)}, bf16[512,16]{0,1:T(8,128)(2,1)}, u32[]{:S(2)}) copy-start(bf16[512,16]{0,1:T(8,128)(2,1)} %get-tuple-element.1648) | copy-start | bytes 49156
  1050.4 19.8 %copy-start.57 = (f32[512]{0:T(512)S(1)}, f32[512]{0:T(512)}, u32[]{:S(2)}) copy-start(f32[512]{0:T(512)} %copy-done.56) | copy-start | bytes 6148
  1052.6 21.4 %copy-start.62 = (f32[1024]{0:T(1024)S(1)}, f32[1024]{0:T(1024)}, u32[]{:S(2)}) copy-start(f32[1024]{0:T(1024)} %get-tuple-element.1513) | copy-start | bytes 12292
  (152 other events, 683.9 us)
Sparse Core Ops, SparseCore 0:
  542.2 70.8 all-reduce.14
  636.5 69.3 all-reduce.18
  708.9 52.4 all-reduce.16
  999.0 71.1 all-reduce.20
Sparse Core Ops, SparseCore 1:
  544.2 27.6 all-gather.7
  573.3 26.8 all-gather.9
  601.6 24.8 all-gather.11
  1024.6 31.6 reduce-scatter.17
  1059.1 31.5 reduce-scatter.9
  1093.6 31.6 reduce-scatter.11
  1128.0 34.4 reduce-scatter.19
  1165.1 34.9 reduce-scatter.13
  1202.8 35.0 reduce-scatter.15
  1240.8 62.7 reduce-scatter.23
  1306.3 63.0 reduce-scatter.21
  1372.3 62.9 reduce-scatter.25
where the time goes:
time: 1460 us; the launch traced here: 1440 us
  waiting for transfers between devices  502 us (34%)
  blocking collectives  291 us (20%)
  other arithmetic  253 us (17%)
  local copies, waits for them, and re-layouts  219 us (15%)
  matrix products  134 us (9%)
  loops' own time  23.2 us (2%)
  between operations  19.9 us (1%)
    dynamic_update_slice x48, other arithmetic, local_core(): lax.scan(block_step, initial, (to_blocks(query_rows), to_blocks(key_vecs)...  89.7 us
    dynamic_slice x88, local copies, waits for them, and re-layouts, local_core(): lax.scan(block_step, initial, (to_blocks(query_rows), to_blocks(key_vecs)...  77.2 us
    dynamic_update_slice x56, local copies, waits for them, and re-layouts, local_core(): lax.scan(block_step, initial, (to_blocks(query_rows), to_blocks(key_vecs)...  66.4 us
    reduce_scatter x1, waiting for transfers between devices, per_device(): lax.psum_scatter(d_w_down, ('dp', 'context'), scatter_dimension=0, tiled=...  65.9 us
    reduce_scatter x1, waiting for transfers between devices, per_device(): lax.psum_scatter(d_w_gate, ('dp', 'context'), scatter_dimension=0, tiled=...  65.8 us
    reduce_scatter x1, waiting for transfers between devices, per_device(): lax.psum_scatter(d_w_up, ('dp', 'context'), scatter_dimension=0, tiled=True)  65.7 us
    psum x1, waiting for transfers between devices, per_device(): residual = hidden_in + lax.psum(attn_part, 'tensor')  52.6 us
    psum x1, waiting for transfers between devices, per_device(): lax.psum(mlp_part.astype(jnp.bfloat16), 'tensor').astype(jnp.float32)  52.1 us
  transfers between devices with their start and end apart: 16, of which 11 were waited for; matrix products, arithmetic and copies ran while one was open for 4% of the time, Pallas kernels for 0%

commit v1 on v0

v1 whole, which is shorter than its diff:
```python
import functools

import jax
import jax.numpy as jnp
from jax import lax
from jax.experimental import pallas as pl
from jax.experimental.pallas import tpu as pltpu
from jax.sharding import PartitionSpec as P

HEAD_K = 128
HEAD_V = 256
TILE = 256

epsilon = 1e-06
gate_divisor = 16.0
highest_precision = lax.Precision.HIGHEST
low = jnp.bfloat16
f32 = jnp.float32
VMEM = pl.BlockSpec(memory_space=pltpu.VMEM)


def mm(a, b, ca=1, cb=0):
    return lax.dot_general(
        a.astype(low), b.astype(low), (((ca,), (cb,)), ((), ())), preferred_element_type=f32
    )


def mm_full(a, b, ca=1, cb=0):
    return lax.dot_general(
        a, b, (((ca,), (cb,)), ((), ())), precision=highest_precision, preferred_element_type=f32
    )


def mask_sum(mask, values):
    hi = values.astype(low)
    rest = values - hi.astype(f32)
    mid = rest.astype(low)
    last = (rest - mid.astype(f32)).astype(low)
    return mm(mask, hi) + mm(mask, mid) + mm(mask, last)


def level_factor(total, half):
    rows, width = total.shape
    if 2 * half >= 16:
        cube = total.reshape(rows // (2 * half), 2 * half, width)
        diff = cube - cube[:, half - 1 : half, :]
    else:
        cube = total.reshape(rows // 8, 8, width)
        sub = lax.broadcasted_iota(jnp.int32, cube.shape, 1)
        mid = cube[:, half - 1 : half, :]
        for block in range(1, 8 // (2 * half)):
            at = block * 2 * half
            mid = jnp.where(sub >= at, cube[:, at + half - 1 : at + half, :], mid)
        diff = cube - mid
    return jnp.exp(jnp.minimum(diff, -diff)).reshape(rows, width)


def small_levels(tile):
    half = tile // 2
    out = []
    while half >= 1:
        out.append(half)
        half //= 2
    return out


def level_mask(half, tile):
    t = lax.broadcasted_iota(jnp.int32, (tile, tile), 0)
    s = lax.broadcasted_iota(jnp.int32, (tile, tile), 1)
    return (t // (2 * half) == s // (2 * half)) & (t % (2 * half) >= half) & (s % (2 * half) < half)


def large_levels(rows, tile):
    half = rows // 2
    out = []
    while half >= tile:
        out.append(half)
        half //= 2
    return out


def local_kernel(heads, proj, rank_out, bias, seg_col, seg_row, out_ref, state_ref, lifted_ref, total_ref, tail_ref):
    rows = proj.shape[0]
    tile = min(TILE, rows)
    kw, vw = heads * HEAD_K, heads * HEAD_V
    rank = rank_out.shape[1]
    rank_act = proj[:, 2 * kw + 2 * vw : 2 * kw + 2 * vw + rank]
    decay = jax.nn.log_sigmoid(mm_full(rank_act, rank_out[...], 1, 1) + bias[...]) / gate_divisor
    segc, segr = seg_col[...], seg_row[...]
    t = lax.broadcasted_iota(jnp.int32, (rows, rows), 0)
    s = lax.broadcasted_iota(jnp.int32, (rows, rows), 1)
    total = mask_sum((t >= s).astype(low), decay)
    total_ref[...] = total
    same = segc == segr
    tail = (segc == segr[:, rows - 1 : rows]).astype(f32)
    for h in range(heads):
        q = proj[:, h * HEAD_K : (h + 1) * HEAD_K] * HEAD_K**-0.5
        k = proj[:, kw + h * HEAD_K : kw + (h + 1) * HEAD_K]
        v = proj[:, 2 * kw + h * HEAD_V : 2 * kw + (h + 1) * HEAD_V].astype(low)
        g = total[:, h * HEAD_K : (h + 1) * HEAD_K]
        diag = jnp.sum(q * k, axis=1, keepdims=True)
        ti = lax.broadcasted_iota(jnp.int32, (tile, tile), 0)
        si = lax.broadcasted_iota(jnp.int32, (tile, tile), 1)
        tiles = rows // tile
        sums = [
            jnp.where(ti == si, diag[i * tile : (i + 1) * tile], 0.0) for i in range(tiles)
        ]
        for half in small_levels(tile):
            factor = level_factor(g, half)
            qh, kh = (q * factor).astype(low), (k * factor).astype(low)
            mask = level_mask(half, tile)
            for i in range(tiles):
                span = slice(i * tile, (i + 1) * tile)
                sums[i] = jnp.where(mask, mm(qh[span], kh[span], 1, 1), sums[i])
        outs = []
        for i in range(tiles):
            span = slice(i * tile, (i + 1) * tile)
            sc = jnp.where(same[span, span] & (ti >= si), sums[i], 0.0)
            outs.append(mm(sc, v[span]))
        for half in large_levels(rows, tile):
            factor = level_factor(g, half)
            qh, kh = (q * factor).astype(low), (k * factor).astype(low)
            for at in range(0, rows, 2 * half):
                right, left = slice(at + half, at + 2 * half), slice(at, at + half)
                sc = jnp.where(same[right, left], mm(qh[right], kh[left], 1, 1), 0.0)
                more = mm(sc, v[left])
                for i in range(half // tile):
                    outs[(at + half) // tile + i] += more[i * tile : (i + 1) * tile]
        for i in range(tiles):
            out_ref[i * tile : (i + 1) * tile, h * HEAD_V : (h + 1) * HEAD_V] = outs[i]
        end = g[rows - 1 : rows]
        kt = k * jnp.exp(end - g) * tail
        state_ref[h] = mm(kt, v, 0, 0)
        lifted_ref[:, h * HEAD_K : (h + 1) * HEAD_K] = (q * jnp.exp(g)).astype(low)
        tail_ref[:, h * HEAD_K : (h + 1) * HEAD_K] = jnp.exp(end)


def intra_back_kernel(heads, proj, total_in, d_mixed, seg_col, seg_row, dq_ref, dk_ref, dv_ref, dg_ref):
    rows = proj.shape[0]
    tile = min(TILE, rows)
    tiles = rows // tile
    kw = heads * HEAD_K
    same = seg_col[...] == seg_row[...]
    ti = lax.broadcasted_iota(jnp.int32, (tile, tile), 0)
    si = lax.broadcasted_iota(jnp.int32, (tile, tile), 1)
    for h in range(heads):
        cols = slice(h * HEAD_K, (h + 1) * HEAD_K)
        vcols = slice(h * HEAD_V, (h + 1) * HEAD_V)
        q = proj[:, cols] * HEAD_K**-0.5
        k = proj[:, kw + h * HEAD_K : kw + (h + 1) * HEAD_K]
        v = proj[:, 2 * kw + h * HEAD_V : 2 * kw + (h + 1) * HEAD_V].astype(low)
        do = d_mixed[:, vcols].astype(low)
        g = total_in[:, cols]
        diag = jnp.sum(q * k, axis=1, keepdims=True)
        d_diag = jnp.sum(do.astype(f32) * v.astype(f32), axis=1, keepdims=True)
        sums = [jnp.where(ti == si, diag[i * tile : (i + 1) * tile], 0.0) for i in range(tiles)]
        allowed = [same[i * tile : (i + 1) * tile, i * tile : (i + 1) * tile] for i in range(tiles)]
        ds = [
            jnp.where(
                allowed[i],
                mm(do[i * tile : (i + 1) * tile], v[i * tile : (i + 1) * tile], 1, 1),
                0.0,
            ).astype(low)
            for i in range(tiles)
        ]
        dq = [(d_diag * k)[i * tile : (i + 1) * tile] for i in range(tiles)]
        dk = [(d_diag * q)[i * tile : (i + 1) * tile] for i in range(tiles)]
        dg = [jnp.zeros((tile, HEAD_K), f32) for i in range(tiles)]
        for half in small_levels(tile):
            factor = level_factor(g, half)
            qh, kh = (q * factor).astype(low), (k * factor).astype(low)
            mask = level_mask(half, tile)
            for i in range(tiles):
                span = slice(i * tile, (i + 1) * tile)
                sums[i] = jnp.where(mask, mm(qh[span], kh[span], 1, 1), sums[i])
                part = jnp.where(mask, ds[i], jnp.zeros((), low))
                dql = mm(part, kh[span])
                dkl = mm(part, qh[span], 0, 0)
                dq[i] += dql * factor[span]
                dk[i] += dkl * factor[span]
                dg[i] += qh[span].astype(f32) * dql - kh[span].astype(f32) * dkl
        dv = []
        for i in range(tiles):
            span = slice(i * tile, (i + 1) * tile)
            sc = jnp.where(allowed[i] & (ti >= si), sums[i], 0.0)
            dv.append(mm(sc, do[span], 0, 0))
        for half in large_levels(rows, tile):
            factor = level_factor(g, half)
            qh, kh = (q * factor).astype(low), (k * factor).astype(low)
            for at in range(0, rows, 2 * half):
                right, left = slice(at + half, at + 2 * half), slice(at, at + half)
                ok = same[right, left]
                sc = jnp.where(ok, mm(qh[right], kh[left], 1, 1), 0.0)
                part = jnp.where(ok, mm(do[right], v[left], 1, 1), 0.0).astype(low)
                dvl = mm(sc, do[right], 0, 0)
                dql = mm(part, kh[left])
                dkl = mm(part, qh[right], 0, 0)
                dgr = qh[right].astype(f32) * dql
                dgl = kh[left].astype(f32) * dkl
                dql = dql * factor[right]
                dkl = dkl * factor[left]
                for i in range(half // tile):
                    piece = slice(i * tile, (i + 1) * tile)
                    r, l = (at + half) // tile + i, at // tile + i
                    dq[r] += dql[piece]
                    dg[r] += dgr[piece]
                    dk[l] += dkl[piece]
                    dg[l] -= dgl[piece]
                    dv[l] += dvl[piece]
        for i in range(tiles):
            span = slice(i * tile, (i + 1) * tile)
            dq_ref[span, cols] = dq[i]
            dk_ref[span, cols] = dk[i]
            dg_ref[span, cols] = dg[i]
            dv_ref[span, vcols] = dv[i]


def silu_parts(gate):
    sig = jax.nn.sigmoid(gate)
    return sig, gate * sig


def mix_kernel(heads, proj, out_local, lifted, reading, prior, gain, mixed_ref, gated_ref):
    kw, vw = heads * HEAD_K, heads * HEAD_V
    for h in range(heads):
        vcols = slice(h * HEAD_V, (h + 1) * HEAD_V)
        mixed = out_local[:, vcols] + reading[...] * mm(
            lifted[:, h * HEAD_K : (h + 1) * HEAD_K], prior[h]
        )
        mixed_ref[:, vcols] = mixed
        rms = lax.rsqrt(jnp.mean(mixed * mixed, axis=1, keepdims=True) + epsilon)
        gate = proj[:, 2 * kw + vw + h * HEAD_V : 2 * kw + vw + (h + 1) * HEAD_V]
        gated_ref[:, vcols] = (mixed * rms * gain[...] * silu_parts(gate)[1]).astype(low)


def gate_back_kernel(heads, proj, mixed_in, d_gated_in, lifted, reading, gain, d_mixed_ref, gate_low_ref, gain_ref, direct_ref):
    kw, vw = heads * HEAD_K, heads * HEAD_V
    gain_sum = jnp.zeros((1, HEAD_V), f32)
    for h in range(heads):
        vcols = slice(h * HEAD_V, (h + 1) * HEAD_V)
        mixed = mixed_in[:, vcols]
        dy = d_gated_in[:, vcols]
        gate = proj[:, 2 * kw + vw + h * HEAD_V : 2 * kw + vw + (h + 1) * HEAD_V]
        sig, act = silu_parts(gate)
        rms = lax.rsqrt(jnp.mean(mixed * mixed, axis=1, keepdims=True) + epsilon)
        unit = mixed * rms
        gate_low_ref[:, vcols] = (
            dy * unit * gain[...] * sig * (1.0 + gate * (1.0 - sig))
        ).astype(low)
        gain_sum += jnp.sum(dy * act * unit, axis=0, keepdims=True)
        e = dy * act * gain[...]
        d_mixed = rms * (e - unit * jnp.mean(e * unit, axis=1, keepdims=True))
        d_mixed = d_mixed.astype(low)
        d_mixed_ref[:, vcols] = d_mixed
        read = lifted[:, h * HEAD_K : (h + 1) * HEAD_K] * reading[...].astype(low)
        direct_ref[h] = mm(read, d_mixed, 0, 0)
    gain_ref[...] = gain_sum


def finish_kernel(heads, rank, proj, total_in, d_mixed, lifted, reading, prior, later, through, rank_out, bias, gate_low, dq_in, dk_in, dv_in, dg_in, seg_col, seg_row, low_ref, rank_out_ref, bias_ref):
    rows = proj.shape[0]
    kw, vw = heads * HEAD_K, heads * HEAD_V
    segc, segr = seg_col[...], seg_row[...]
    t = lax.broadcasted_iota(jnp.int32, (rows, rows), 0)
    s = lax.broadcasted_iota(jnp.int32, (rows, rows), 1)
    suffix = ((t <= s) & (segc == segr)).astype(low)
    tail = (segc == segr[:, rows - 1 : rows]).astype(f32)
    read = reading[...]
    base = 2 * kw + 2 * vw
    rank_act = proj[:, base : base + rank]
    pre = mm_full(rank_act, rank_out[...], 1, 1) + bias[...]
    rank_part = jnp.zeros((rows, rank), f32)
    for h in range(heads):
        cols = slice(h * HEAD_K, (h + 1) * HEAD_K)
        vcols = slice(h * HEAD_V, (h + 1) * HEAD_V)
        k = proj[:, kw + h * HEAD_K : kw + (h + 1) * HEAD_K]
        v = proj[:, 2 * kw + h * HEAD_V : 2 * kw + (h + 1) * HEAD_V].astype(low)
        do = d_mixed[:, vcols]
        g = total_in[:, cols]
        end = g[rows - 1 : rows]
        pulled = mm(do, prior[h], 1, 1) * read
        dq = dq_in[:, cols] + pulled * jnp.exp(g)
        fall = jnp.exp(end - g) * tail
        kt = (k * fall).astype(low)
        dkt = mm(v, later[h], 1, 1)
        dk = dk_in[:, cols] + dkt * fall
        crossing = kt.astype(f32) * dkt
        dv = dv_in[:, vcols] + mm(kt, later[h])
        dg = dg_in[:, cols] + pulled * lifted[:, cols].astype(f32) - crossing
        across = jnp.sum(crossing, axis=0, keepdims=True) + through[:, cols]
        d_decay = mask_sum(suffix, dg) + tail * across
        d_pre = d_decay * jax.nn.sigmoid(-pre[:, cols]) / gate_divisor
        low_ref[:, cols] = (dq * HEAD_K**-0.5).astype(low)
        low_ref[:, kw + h * HEAD_K : kw + (h + 1) * HEAD_K] = dk.astype(low)
        low_ref[:, 2 * kw + h * HEAD_V : 2 * kw + (h + 1) * HEAD_V] = dv.astype(low)
        rank_part += mm_full(d_pre, rank_out[cols, :])
        rank_out_ref[cols, :] = mm_full(d_pre, rank_act, 0, 0)
        bias_ref[:, cols] = jnp.sum(d_pre, axis=0, keepdims=True)
    low_ref[:, 2 * kw + vw : base] = gate_low[...]
    wide = low_ref.shape[1] - base
    low_ref[:, base:] = jnp.concatenate(
        [rank_part, jnp.zeros((rows, wide - rank), f32)], axis=1
    ).astype(low)


def call(kernel, outs, *args):
    return pl.pallas_call(
        kernel,
        out_shape=[jax.ShapeDtypeStruct(shape, kind) for shape, kind in outs],
        in_specs=[VMEM] * len(args),
        out_specs=[VMEM] * len(outs),
        compiler_params=pltpu.CompilerParams(vmem_limit_bytes=56 * 1024 * 1024),
    )(*args)


def norm_back(scaled_grad, unit_rows, rstd_rows):
    return rstd_rows * (
        scaled_grad - unit_rows * jnp.mean(scaled_grad * unit_rows, axis=-1, keepdims=True)
    )


def gather(value):
    return lax.all_gather(value, ("dp", "context"), axis=0, tiled=True)


def scatter(value):
    return lax.psum_scatter(value, ("dp", "context"), scatter_dimension=0, tiled=True)


def dot32(a, b, ca=1, cb=0):
    return lax.dot_general(a, b, (((ca,), (cb,)), ((), ())), preferred_element_type=f32)


def chain(factors, values):
    weight = jnp.ones_like(factors[0])
    out = jnp.zeros_like(values[0])
    for j in reversed(range(factors.shape[0])):
        out = out + weight[..., None] * values[j]
        weight = weight * factors[j]
    return out


def per_device(
    block_in, segments, cotangent, norm_gain, w_query, w_key, w_value, w_gate_out, w_rank_in,
    w_rank_out, gate_bias, group_gain, w_output, mlp_gain, w_gate, w_up, w_down,
):
    hidden_in, seg, grad_out = block_in[0], segments[0], cotangent[0]
    tokens, width = hidden_in.shape
    rank = w_rank_in.shape[1]
    heads = w_rank_out.shape[0] // HEAD_K
    kw, vw = heads * HEAD_K, heads * HEAD_V
    base = 2 * kw + 2 * vw
    rest = -(rank + 2) % 128 + rank + 2
    rows_here = w_query.shape[0]
    seg_col, seg_row = seg[:, None], seg[None, :]
    bias = gate_bias[None, :]
    gain_g = group_gain[None, :]

    packed = jnp.concatenate(
        [
            w_query, w_key, w_value, w_gate_out, w_rank_in, norm_gain[:, None], mlp_gain[:, None],
            jnp.zeros((rows_here, rest - rank - 2), low), w_output,
        ],
        axis=1,
    )
    mixer = gather(packed)
    gate_w, up_w, down_w = gather(w_gate), gather(w_up), gather(w_down)
    wide = base + rest
    w_in = mixer[:, :wide]
    w_out = mixer[:, wide:]
    gain_one = mixer[:, base + rank].astype(f32)
    gain_two = mixer[:, base + rank + 1].astype(f32)

    rstd_one = lax.rsqrt(jnp.mean(hidden_in * hidden_in, axis=-1, keepdims=True) + epsilon)
    unit_one = hidden_in * rstd_one
    normed_one = (unit_one * gain_one).astype(low)
    proj = dot32(normed_one, w_in)
    out_local, state_local, lifted, total, ends = call(
        functools.partial(local_kernel, heads),
        [
            ((tokens, vw), f32), ((heads, HEAD_K, HEAD_V), f32), ((tokens, kw), low),
            ((tokens, kw), f32), ((1, kw), f32),
        ],
        proj, w_rank_out, bias, seg_col, seg_row,
    )
    peers, here = lax.axis_size("context"), lax.axis_index("context")
    firsts = lax.all_gather(jnp.stack([seg[0], seg[-1]]).astype(f32), "context")
    states = lax.all_gather(
        jnp.concatenate(
            [
                state_local.reshape(kw, HEAD_V),
                jnp.broadcast_to(ends.reshape(kw, 1), (kw, 128)),
            ],
            axis=1,
        ),
        "context",
    )
    order = jnp.arange(peers)
    first, last = firsts[:, 0], firsts[:, 1]
    before = jnp.concatenate([jnp.full((1,), -1.0, f32), last[:-1]])
    keep = jnp.where((first == before) | (before < 0.0), 1.0, 0.0)
    unbroken = jnp.where(first == last, 1.0, 0.0)
    decays = states[:, :, HEAD_V].reshape(peers, heads, HEAD_K)
    spans = decays * unbroken[:, None, None]
    passing = spans * keep[:, None, None]
    earlier = (order < here)[:, None, None]
    prior = chain(
        jnp.where(earlier, passing, 1.0),
        jnp.where(earlier[..., None], states[:, :, :HEAD_V].reshape(peers, heads, HEAD_K, HEAD_V), 0.0),
    )
    prior_last = jnp.where(here > 0, before[here], -1.0)
    reading = (seg.astype(f32) == prior_last).astype(f32)[:, None]

    mixed, gated = call(
        functools.partial(mix_kernel, heads),
        [((tokens, vw), f32), ((tokens, vw), low)],
        proj, out_local, lifted, reading, prior, gain_g,
    )
    attn = lax.psum(dot32(gated, w_out, 1, 1).astype(low), "tensor")
    residual = hidden_in + attn.astype(f32)
    rstd_two = lax.rsqrt(jnp.mean(residual * residual, axis=-1, keepdims=True) + epsilon)
    unit_two = residual * rstd_two
    normed_two = (unit_two * gain_two).astype(low)
    gate_pre = dot32(normed_two, gate_w)
    up_value = dot32(normed_two, up_w)
    sig = jax.nn.sigmoid(gate_pre)
    activation = (gate_pre * sig * up_value).astype(low)
    grad_low = grad_out.astype(low)
    d_activation = dot32(grad_low, down_w)
    d_gate_pre = (d_activation * up_value * sig * (1.0 + gate_pre * (1.0 - sig))).astype(low)
    d_up_value = (d_activation * gate_pre * sig).astype(low)
    dnormed_two = lax.psum(
        (dot32(d_gate_pre, gate_w, 1, 1) + dot32(d_up_value, up_w, 1, 1)).astype(low), "tensor"
    ).astype(f32)
    block_out = residual + lax.psum(
        dot32(activation, down_w, 1, 1).astype(low), "tensor"
    ).astype(f32)
    d_w_down = scatter(dot32(grad_low, activation, 0, 0).astype(low))
    d_w_gate = scatter(dot32(normed_two, d_gate_pre, 0, 0).astype(low))
    d_w_up = scatter(dot32(normed_two, d_up_value, 0, 0).astype(low))

    d_mlp_gain = jnp.sum(dnormed_two * unit_two, axis=0)
    d_residual = grad_out + norm_back(dnormed_two * gain_two, unit_two, rstd_two)
    residual_low = d_residual.astype(low)
    d_gated = dot32(residual_low, w_out)
    d_mixed, gate_low, gain_part, direct = call(
        functools.partial(gate_back_kernel, heads),
        [
            ((tokens, vw), low), ((tokens, vw), low), ((1, HEAD_V), f32),
            ((heads, HEAD_K, HEAD_V), f32),
        ],
        proj, mixed, d_gated, lifted, reading, gain_g,
    )
    directs = lax.all_gather(direct.astype(low), "context")
    dq, dk, dv, dg = call(
        functools.partial(intra_back_kernel, heads),
        [
            ((tokens, kw), f32), ((tokens, kw), f32), ((tokens, vw), f32), ((tokens, kw), f32),
        ],
        proj, total, d_mixed, seg_col, seg_row,
    )
    after = (order > here)[:, None, None]
    later = chain(
        jnp.where(after, passing, 1.0)[::-1],
        jnp.where(after[..., None], directs.astype(f32), 0.0)[::-1],
    )
    through = passing[here] * jnp.sum(prior * later, axis=-1)
    low_all, rank_out_part, bias_part = call(
        functools.partial(finish_kernel, heads, rank),
        [((tokens, wide), low), ((kw, rank), f32), ((1, kw), f32)],
        proj, total, d_mixed, lifted, reading, prior, later, through.reshape(1, kw), w_rank_out,
        bias, gate_low, dq, dk, dv, dg, seg_col, seg_row,
    )
    dnormed_one = lax.psum(dot32(low_all, w_in, 1, 1).astype(low), "tensor").astype(f32)
    d_w_in = scatter(
        jnp.concatenate(
            [dot32(normed_one, low_all, 0, 0).astype(low), dot32(residual_low, gated, 0, 0).astype(low)],
            axis=1,
        )
    ).astype(f32)
    d_norm_gain = jnp.sum(dnormed_one * unit_one, axis=0)
    d_block_in = d_residual + norm_back(dnormed_one * gain_one, unit_one, rstd_one)
    gains = scatter(jnp.stack([d_norm_gain, d_mlp_gain], axis=1))
    d_rank_in = lax.psum(d_w_in[:, base : base + rank], "tensor")
    small = lax.psum(
        jnp.concatenate([rank_out_part.reshape(-1), bias_part[0]]), ("dp", "context")
    )
    d_group = lax.psum(gain_part[0], ("dp", "context", "tensor"))
    return (
        block_out[None],
        d_block_in[None],
        gains[:, 0],
        d_w_in[:, :kw],
        d_w_in[:, kw : 2 * kw],
        d_w_in[:, 2 * kw : 2 * kw + vw],
        d_w_in[:, 2 * kw + vw : base],
        d_rank_in,
        small[: kw * rank].reshape(kw, rank),
        small[kw * rank :],
        d_group,
        d_w_in[:, wide:],
        gains[:, 1],
        d_w_gate.astype(f32),
        d_w_up.astype(f32),
        d_w_down.astype(f32),
    )


def solution(mesh):
    placed = (
        P("dp", "context", None),
        P("dp", "context"),
        P("dp", "context", None),
        P(("dp", "context")),
        P(("dp", "context"), "tensor"),
        P(("dp", "context"), "tensor"),
        P(("dp", "context"), "tensor"),
        P(("dp", "context"), "tensor"),
        P(("dp", "context"), None),
        P("tensor", None),
        P("tensor"),
        P(),
        P(("dp", "context"), "tensor"),
        P(("dp", "context")),
        P(("dp", "context"), "tensor"),
        P(("dp", "context"), "tensor"),
        P(("dp", "context"), "tensor"),
    )
    return jax.shard_map(
        per_device,
        mesh=mesh,
        in_specs=placed,
        out_specs=(
            P("dp", "context", None),
            P("dp", "context", None),
            P(("dp", "context")),
            P(("dp", "context"), "tensor"),
            P(("dp", "context"), "tensor"),
            P(("dp", "context"), "tensor"),
            P(("dp", "context"), "tensor"),
            P(("dp", "context"), None),
            P("tensor", None),
            P("tensor"),
            P(),
            P(("dp", "context"), "tensor"),
            P(("dp", "context")),
            P(("dp", "context"), "tensor"),
            P(("dp", "context"), "tensor"),
            P(("dp", "context"), "tensor"),
        ),
        check_vma=False,
    )
```

time: 1460 us -> 627 us (0.43); the launches traced: 1440 us -> 626 us
  other arithmetic: 253 us -> 28.4 us
  local copies, waits for them, and re-layouts: 219 us -> 37.4 us
  blocking collectives: 291 us -> 125 us
  waiting for transfers between devices: 502 us -> 355 us
  matrix products: 134 us -> 41.7 us
  loops' own time: 23.2 us -> 0 us
  Pallas kernels: 0 us -> 22.7 us
    reduce_scatter x9 -> x0, waiting for transfers between devices: 326 us -> none  [the longest x1 65.9 us: per_device(): lax.psum_scatter(d_w_down, ('dp', 'context'), scatter_dimension=0, tiled=...]
    all_gather x12 -> x3, blocking collectives: 234 us -> 44.5 us  [the longest x1 17.9 us: per_device(): lax.all_gather(jnp.concatenate([state_local.reshape(kw, HEAD_V), jnp.broa...]
    unnamed x16 -> x17, waiting for transfers between devices: 1.79 us -> 123 us
    dot_general x105 -> x15, matrix products: 134 us -> 41.7 us  [dot32(): lax.dot_general(a, b, (((ca,), (cb,)), ((), ())), preferred_element_type=...]
    dynamic_update_slice x48 -> x0, other arithmetic: 89.7 us -> none  [local_core(): lax.scan(block_step, initial, (to_blocks(query_rows), to_blocks(key_vecs)...]
    dynamic_slice x96 -> x1, local copies, waits for them, and re-layouts: 81.9 us -> 0.58 us  [per_device(): prior_last = jnp.where(here > 0, before[here], -1.0)]
    all_gather x3 -> x4, waiting for transfers between devices: 0.01 us -> 81.1 us  [gather(): return lax.all_gather(value, ('dp', 'context'), axis=0, tiled=True)]
    dynamic_update_slice x56 -> x0, local copies, waits for them, and re-layouts: 66.4 us -> none  [local_core(): lax.scan(block_step, initial, (to_blocks(query_rows), to_blocks(key_vecs)...]
  transfers between devices with their start and end apart: 16 -> 12, of which waited for: 11 -> 11; matrix products, arithmetic and copies ran while one was open for 4% -> 10% of each run, Pallas kernels for 0% -> 0%
where the time goes in v1:
time: 627 us; the launch traced here: 626 us
  waiting for transfers between devices  355 us (57%)
  blocking collectives  125 us (20%)
  matrix products  41.7 us (7%)
  local copies, waits for them, and re-layouts  37.4 us (6%)
  other arithmetic  28.4 us (5%)
  Pallas kernels  22.7 us (4%)
  between operations  15.2 us (2%)
    unnamed x17, waiting for transfers between devices  123 us
    all_gather x4, waiting for transfers between devices, gather(): return lax.all_gather(value, ('dp', 'context'), axis=0, tiled=True)  81.1 us
    psum x1, waiting for transfers between devices, per_device(): lax.psum(dot32(activation, down_w, 1, 1).astype(low), 'tensor').astype(f32)  52.6 us
    psum x1, waiting for transfers between devices, per_device(): attn = lax.psum(dot32(gated, w_out, 1, 1).astype(low), 'tensor')  50.1 us
    psum x1, waiting for transfers between devices, per_device(): lax.psum((dot32(d_gate_pre, gate_w, 1, 1) + dot32(d_up_value, up_w, 1, 1)...  47.6 us
    dot_general x15, matrix products, dot32(): lax.dot_general(a, b, (((ca,), (cb,)), ((), ())), preferred_element_type=...  41.7 us
    psum x1, blocking collectives, per_device(): d_group = lax.psum(gain_part[0], ('dp', 'context', 'tensor'))  38.5 us
    psum x1, blocking collectives, per_device(): lax.psum(jnp.concatenate([rank_out_part.reshape(-1), bias_part[0]]), ('dp...  31.3 us
  transfers between devices with their start and end apart: 12, of which 11 were waited for; matrix products, arithmetic and copies ran while one was open for 10% of the time, Pallas kernels for 0%

profile of v1, /device:TPU:0, one launch (start us, length us, event | category | flops | bytes accessed | tf_op | source)
XLA Modules:
  0.0 625.6 jit_solution(2088404885439841309)
XLA Ops:
  9.6 1.9 concatenate.29
  14.2 12.7 %all-gather.2 = f32[4,1,2]{2,1,0:T(1,128)S(1)} all-gather(f32[1,1,2]{2,1,0:T(1,128)S(1)} %fusion.38), channel_id=1, replica_groups=mesh['dp'=2,'context'=4,'tensor'=4] {'context'}, dimensions={0}, use_global_device_ids=true | all-gather | bytes 40 | tf_op jit(solution)/shard_map/all_gather | solution.py:387
  31.4 1.5 copy.80.seg_col
  33.0 1.8 fusion.13
  34.8 11.1 %all-gather.8.cloned.1.call-done = bf16[1024,1152]{1,0:T(8,128)(2,1)} async-done(((bf16[128,1152]{1,0:T(8,128)(2,1)}), bf16[1024,1152]{1,0:T(8,128)(2,1)}) %all-gather.8.cloned.1.call-update) | async-done | bytes 2359312 | tf_op jit(solution)/shard_map/all_gather | solution.py:323
  45.9 1.5 convert_reduce_fusion
  47.4 4.0 fusion.16.proj
  51.5 5.6 shard_map.288
  58.7 17.9 %all-gather = f32[512,384]{1,0:T(8,128)S(1)} all-gather(f32[128,384]{1,0:T(8,128)S(1)} %pad_maximum_fusion.1), channel_id=2, replica_groups=mesh['dp'=2,'context'=4,'tensor'=4] {'context'}, dimensions={0}, use_global_device_ids=true | all-gather | bytes 983040 | tf_op jit(solution)/shard_map/all_gather | solution.py:388
  77.9 2.9 shard_map.289
  80.7 2.6 convolution_convert_fusion.5
  85.3 50.1 %all-reduce.5.cloned.1.call-done = bf16[512,1024]{1,0:T(8,128)(2,1)} async-done(((bf16[512,1024]{1,0:T(8,128)(2,1)}), bf16[512,1024]{1,0:T(8,128)(2,1)}) %all-reduce.5.cloned.1.call-update) | async-done | bytes 1048592 | tf_op jit(solution)/shard_map/psum | solution.py:419
  135.4 2.3 multiply_reduce_fusion
  139.0 24.5 %all-gather.12.cloned.1.call-done = bf16[1024,704]{0,1:T(8,128)(2,1)} async-done(((bf16[128,704]{0,1:T(8,128)(2,1)}), bf16[1024,704]{0,1:T(8,128)(2,1)}) %all-gather.12.cloned.1.call-update) | async-done | bytes 1441808 | tf_op jit(solution)/shard_map/all_gather | solution.py:323
  163.5 3.7 fusion.52
  167.2 22.7 %all-gather.10.cloned.1.call-done = bf16[1024,704]{0,1:T(8,128)(2,1)} async-done(((bf16[128,704]{0,1:T(8,128)(2,1)}), bf16[1024,704]{0,1:T(8,128)(2,1)}) %all-gather.10.cloned.1.call-update) | async-done | bytes 1441808 | tf_op jit(solution)/shard_map/all_gather | solution.py:323
  190.0 3.7 fusion.51
  193.7 22.7 %all-gather.14.cloned.1.call-done = bf16[1024,704]{0,1:T(8,128)(2,1)} async-done(((bf16[128,704]{0,1:T(8,128)(2,1)}), bf16[1024,704]{0,1:T(8,128)(2,1)}) %all-gather.14.cloned.1.call-update) | async-done | bytes 1441808 | tf_op jit(solution)/shard_map/all_gather | solution.py:323
  216.5 4.4 multiply_convert_fusion.2
  223.1 2.0 add_convert_fusion
  225.4 3.3 convolution_convert_fusion.4
  228.7 47.6 %all-reduce.7.cloned.1.call-done = bf16[512,1024]{1,0:T(8,128)(2,1)} async-done(((bf16[512,1024]{1,0:T(8,128)(2,1)}), bf16[512,1024]{1,0:T(8,128)(2,1)}) %all-reduce.7.cloned.1.call-update) | async-done | bytes 1048592 | tf_op jit(solution)/shard_map/psum | solution.py:432
  276.3 2.1 fusion.11
  281.6 3.2 shard_map.290
  285.7 13.8 %all-gather.1 = bf16[4,128,256]{2,1,0:T(8,128)(2,1)S(1)} all-gather(bf16[1,128,256]{2,1,0:T(8,128)(2,1)S(1)} %convert_element_type.151), channel_id=3, replica_groups=mesh['dp'=2,'context'=4,'tensor'=4] {'context'}, dimensions={0}, use_global_device_ids=true | all-gather | bytes 327680 | tf_op jit(solution)/shard_map/all_gather | solution.py:454
  301.0 6.0 shard_map.291
  307.0 5.0 shard_map.292
  312.0 3.4 fusion.18
  315.5 2.4 convolution_convert_fusion.1
  317.9 1.6 copy.99
  319.6 2.4 convolution_convert_fusion.2
  321.9 1.6 copy.97
  323.8 2.7 fusion.21
  326.5 1.7 copy.101
  328.3 2.2 convolution_convert_fusion.6
  330.8 2.5 convolution_convert_fusion
  333.3 52.6 %all-reduce.9.cloned.1.call-done = (bf16[512,1024]{1,0:T(8,128)(2,1)}, bf16[512,1024]{1,0:T(8,128)(2,1)}) async-done(((bf16[512,1024]{1,0:T(8,128)(2,1)}, bf16[512,1024]{1,0:T(8,128)(2,1)}), (bf16[512,1024]{1,0:T(8,128)(2,1)}, bf16[512,1024]{1,0:T(8,128)(2,1)})) %all-reduce.9.cloned.1.call-update) | async-done | bytes 2097168 | tf_op jit(solution)/shard_map/psum | solution.py:435
  385.9 2.6 fusion.12
  389.6 3.1 pad_maximum_fusion
  392.7 4.3 copy.95
  398.0 31.3 %psum.54 = f32[2176]{0:T(1024)S(1)} all-reduce(f32[2176]{0:T(1024)S(1)} %pad_maximum_fusion.2), channel_id=1, replica_groups=mesh['dp'=2,'context'=4,'tensor'=4] {'dp','context'}, use_global_device_ids=true, to_apply=%region_14.15 | all-reduce | flops 2176 | bytes 17408 | tf_op jit(solution)/shard_map/psum | solution.py:485
  430.6 38.5 %psum.55 = f32[256]{0:T(256)} all-reduce(f32[256]{0:T(256)S(1)} %bitcast.171), channel_id=1, replica_groups=mesh['dp'=2,'context'=4,'tensor'=4] {'dp','context','tensor'}, use_global_device_ids=true, to_apply=%region_15.16 | all-reduce | flops 256 | bytes 2048 | tf_op jit(solution)/shard_map/psum | solution.py:488
  473.5 39.8 %reduce-scatter.24.cloned.1.call-done = bf16[128,704]{1,0:T(8,128)(2,1)} async-done(((bf16[1024,704]{1,0:T(8,128)(2,1)}), bf16[128,704]{1,0:T(8,128)(2,1)}) %reduce-scatter.24.cloned.1.call-update) | async-done | bytes 180240
  515.2 1.6 add_bitcast_fusion
  518.4 1.9 fusion.7
  520.3 28.3 %reduce-scatter.16.cloned.1.call-done = f32[128,2]{1,0:T(8,128)} async-done(((f32[1024,2]{1,0:T(8,128)}), f32[128,2]{1,0:T(8,128)}) %reduce-scatter.16.cloned.1.call-update) | async-done | bytes 1040
  550.7 52.6 %reduce-scatter.18.cloned.1.call-done = bf16[128,1152]{1,0:T(8,128)(2,1)} async-done(((bf16[1024,1152]{1,0:T(8,128)(2,1)}), bf16[128,1152]{1,0:T(8,128)(2,1)}) %reduce-scatter.18.cloned.1.call-update) | async-done | bytes 294928
  604.5 10.6 %psum.53 = f32[128,16]{0,1:T(8,128)} all-reduce(f32[128,16]{0,1:T(8,128)S(1)} %slice.185), channel_id=1, replica_groups=mesh['dp'=2,'context'=4,'tensor'=4] {'tensor'}, use_global_device_ids=true, to_apply=%region_13.14 | all-reduce | flops 2048 | bytes 16384 | tf_op jit(solution)/shard_map/psum | solution.py:484
  (128 shorter events, 42.0 us)
Async XLA Ops:
  7.2 38.7 %all-gather.8.cloned.1.call-start = ((), (), s32[]{:S(2)}) async-start(), calls=%async_computation.5 | async-start | bytes 2654208 | tf_op jit(solution)/shard_map/all_gather | solution.py:323
  9.6 37.8 %copy-start = (f32[1,512,1024]{2,1,0:T(8,128)S(1)}, f32[1,512,1024]{2,1,0:T(8,128)}, u32[]{:S(2)}) copy-start(f32[1,512,1024]{2,1,0:T(8,128)} %param.17) | copy-start | bytes 6291460
  11.6 123.9 %all-reduce.5.cloned.1.call-start = ((), (), s32[]{:S(2)}) async-start(), calls=%async_computation.6 | async-start | bytes 2097152 | tf_op jit(solution)/shard_map/psum | solution.py:419
  83.3 80.2 %all-gather.12.cloned.1.call-start = ((), (), s32[]{:S(2)}) async-start(), calls=%async_computation.8 | async-start | bytes 1622016 | tf_op jit(solution)/shard_map/all_gather | solution.py:323
  84.1 105.9 %all-gather.10.cloned.1.call-start = ((), (), s32[]{:S(2)}) async-start(), calls=%async_computation.7 | async-start | bytes 1622016 | tf_op jit(solution)/shard_map/all_gather | solution.py:323
  84.6 131.8 %all-gather.14.cloned.1.call-start = ((), (), s32[]{:S(2)}) async-start(), calls=%async_computation.9 | async-start | bytes 1622016 | tf_op jit(solution)/shard_map/all_gather | solution.py:323
  85.2 191.0 %all-reduce.7.cloned.1.call-start = ((), (), s32[]{:S(2)}) async-start(), calls=%async_computation.10 | async-start | bytes 2097152 | tf_op jit(solution)/shard_map/psum | solution.py:432
  216.5 4.5 copy-start.15
  220.9 1.1 copy-start.18
  220.9 1.1 copy-start.17
  220.9 4.4 copy-start.10
  221.0 2.1 copy-start.14
  225.1 160.7 %all-reduce.9.cloned.1.call-start = ((), (), s32[]{:S(2)}) async-start(), calls=%async_computation.16 | async-start | bytes 4194304 | tf_op jit(solution)/shard_map/psum | solution.py:435
  276.3 2.1 copy-start.5
  276.3 2.2 copy-start.7
  278.4 1.9 copy-start.9
  279.0 1.3 copy-start.3
  315.5 153.6 %reduce-scatter.22.cloned.1.call-start = ((), (), s32[]{:S(2)}) async-start(), calls=%async_computation.14 | async-start | bytes 1769472
  319.5 152.2 %reduce-scatter.20.cloned.1.call-start = ((), (), s32[]{:S(2)}) async-start(), calls=%async_computation.13 | async-start | bytes 1769472
  323.5 189.8 %reduce-scatter.24.cloned.1.call-start = ((), (), s32[]{:S(2)}) async-start(), calls=%async_computation.15 | async-start | bytes 1769472
  328.2 2.3 copy-start.16
  328.2 220.3 %reduce-scatter.16.cloned.1.call-start = ((), (), s32[]{:S(2)}) async-start(), calls=%async_computation.11 | async-start | bytes 589824
  328.3 2.5 copy-start.1
  389.6 213.7 %reduce-scatter.18.cloned.1.call-start = ((), (), s32[]{:S(2)}) async-start(), calls=%async_computation.12 | async-start | bytes 2654208
  397.1 0.8 copy-start.11
  397.1 0.9 copy-start.13
  397.1 33.5 %copy-start.12 = (f32[1,256]{1,0:T(1,128)S(1)}, f32[1,256]{1,0:T(1,128)}, u32[]{:S(2)}) copy-start(f32[1,256]{1,0:T(1,128)} %get-tuple-element.51) | copy-start | bytes 3076
  397.1 118.1 %copy-start.8 = (bf16[512,1024]{1,0:T(8,128)(2,1)S(1)}, bf16[512,1024]{1,0:T(8,128)(2,1)}, u32[]{:S(2)}) copy-start(bf16[512,1024]{1,0:T(8,128)(2,1)} %get-tuple-element.122) | copy-start | bytes 3145732
  515.2 2.3 copy-start.2
  515.2 3.0 copy-start.4
  515.2 3.2 copy-start.6
Sparse Core Ops, SparseCore 0:
  11.7 34.1 all-gather.7
  83.5 51.9 all-reduce.4
  137.0 26.4 all-gather.11
  164.9 24.9 all-gather.9
  191.4 24.9 all-gather.13
  225.2 50.9 all-reduce.6
  315.6 70.1 all-reduce.8
  388.2 40.5 reduce-scatter.21
  431.0 40.5 reduce-scatter.19
  473.8 39.4 reduce-scatter.23
  515.6 32.9 reduce-scatter.15
  550.7 52.5 reduce-scatter.17

commit v2 on v1

--- a/solution.py
+++ b/solution.py
@@ -16,6 +16,7 @@
 highest_precision = lax.Precision.HIGHEST
 low = jnp.bfloat16
 f32 = jnp.float32
+MESH = pl.DeviceIdType.MESH
 VMEM = pl.BlockSpec(memory_space=pltpu.VMEM)
 
 
@@ -313,6 +314,74 @@
     )(*args)
 
 
+def sum_kernel(n, x_ref, out_ref, arrived, total, send_sem, recv_sem, back_send, back_recv):
+    me = lax.axis_index("tensor")
+    rows = x_ref.shape[0] // n
+    barrier = pltpu.get_barrier_semaphore()
+    for d in range(1, n):
+        pl.semaphore_signal(
+            barrier, inc=1, device_id={"tensor": lax.rem(me + d, n)}, device_id_type=MESH
+        )
+    pl.semaphore_wait(barrier, n - 1)
+    sends = []
+    for d in range(1, n):
+        peer = lax.rem(me + d, n)
+        copy = pltpu.make_async_remote_copy(
+            src_ref=x_ref.at[pl.ds(pl.multiple_of(peer * rows, rows), rows)],
+            dst_ref=arrived.at[d - 1],
+            send_sem=send_sem.at[d - 1],
+            recv_sem=recv_sem.at[d - 1],
+            device_id={"tensor": peer},
+            device_id_type=MESH,
+        )
+        copy.start()
+        sends.append(copy)
+    mine = pl.ds(pl.multiple_of(me * rows, rows), rows)
+    value = x_ref[mine, :].astype(f32)
+    for d in range(1, n):
+        sends[d - 1].wait_recv()
+        value = value + arrived[d - 1].astype(f32)
+    total[...] = value.astype(low)
+    backs = []
+    for d in range(1, n):
+        copy = pltpu.make_async_remote_copy(
+            src_ref=total,
+            dst_ref=out_ref.at[mine],
+            send_sem=back_send.at[d - 1],
+            recv_sem=back_recv.at[d - 1],
+            device_id={"tensor": lax.rem(me + d, n)},
+            device_id_type=MESH,
+        )
+        copy.start()
+        backs.append(copy)
+    out_ref[mine, :] = value.astype(low)
+    for d in range(1, n):
+        sends[d - 1].wait_send()
+        backs[d - 1].wait()
+
+
+def tensor_sum(x):
+    n = lax.axis_size("tensor")
+    rows = x.shape[0] // n
+    return pl.pallas_call(
+        functools.partial(sum_kernel, n),
+        out_shape=jax.ShapeDtypeStruct(x.shape, x.dtype),
+        in_specs=[VMEM],
+        out_specs=VMEM,
+        scratch_shapes=[
+            pltpu.VMEM((n - 1, rows, x.shape[1]), x.dtype),
+            pltpu.VMEM((rows, x.shape[1]), x.dtype),
+            pltpu.SemaphoreType.DMA((n - 1,)),
+            pltpu.SemaphoreType.DMA((n - 1,)),
+            pltpu.SemaphoreType.DMA((n - 1,)),
+            pltpu.SemaphoreType.DMA((n - 1,)),
+        ],
+        compiler_params=pltpu.CompilerParams(
+            collective_id=0, has_side_effects=True, vmem_limit_bytes=32 * 1024 * 1024
+        ),
+    )(x)
+
+
 def norm_back(scaled_grad, unit_rows, rstd_rows):
     return rstd_rows * (
         scaled_grad - unit_rows * jnp.mean(scaled_grad * unit_rows, axis=-1, keepdims=True)
@@ -324,7 +393,9 @@
 
 
 def scatter(value):
-    return lax.psum_scatter(value, ("dp", "context"), scatter_dimension=0, tiled=True)
+    for axis in ("dp", "context"):
+        value = lax.psum_scatter(value, axis, scatter_dimension=0, tiled=True)
+    return value
 
 
 def dot32(a, b, ca=1, cb=0):
@@ -364,7 +435,9 @@
         axis=1,
     )
     mixer = gather(packed)
-    gate_w, up_w, down_w = gather(w_gate), gather(w_up), gather(w_down)
+    hidden = w_gate.shape[1]
+    mlp = gather(jnp.concatenate([w_gate, w_up, w_down], axis=1))
+    gate_w, up_w, down_w = mlp[:, :hidden], mlp[:, hidden : 2 * hidden], mlp[:, 2 * hidden :]
     wide = base + rest
     w_in = mixer[:, :wide]
     w_out = mixer[:, wide:]
@@ -416,7 +489,7 @@
         [((tokens, vw), f32), ((tokens, vw), low)],
         proj, out_local, lifted, reading, prior, gain_g,
     )
-    attn = lax.psum(dot32(gated, w_out, 1, 1).astype(low), "tensor")
+    attn = tensor_sum(dot32(gated, w_out, 1, 1).astype(low))
     residual = hidden_in + attn.astype(f32)
     rstd_two = lax.rsqrt(jnp.mean(residual * residual, axis=-1, keepdims=True) + epsilon)
     unit_two = residual * rstd_two
@@ -429,15 +502,20 @@
     d_activation = dot32(grad_low, down_w)
     d_gate_pre = (d_activation * up_value * sig * (1.0 + gate_pre * (1.0 - sig))).astype(low)
     d_up_value = (d_activation * gate_pre * sig).astype(low)
-    dnormed_two = lax.psum(
-        (dot32(d_gate_pre, gate_w, 1, 1) + dot32(d_up_value, up_w, 1, 1)).astype(low), "tensor"
+    dnormed_two = tensor_sum(
+        (dot32(d_gate_pre, gate_w, 1, 1) + dot32(d_up_value, up_w, 1, 1)).astype(low)
     ).astype(f32)
-    block_out = residual + lax.psum(
-        dot32(activation, down_w, 1, 1).astype(low), "tensor"
+    mlp_part = dot32(activation, down_w, 1, 1).astype(low)
+    d_mlp = scatter(
+        jnp.concatenate(
+            [
+                dot32(normed_two, d_gate_pre, 0, 0).astype(low),
+                dot32(normed_two, d_up_value, 0, 0).astype(low),
+                dot32(grad_low, activation, 0, 0).astype(low),
+            ],
+            axis=1,
+        )
     ).astype(f32)
-    d_w_down = scatter(dot32(grad_low, activation, 0, 0).astype(low))
-    d_w_gate = scatter(dot32(normed_two, d_gate_pre, 0, 0).astype(low))
-    d_w_up = scatter(dot32(normed_two, d_up_value, 0, 0).astype(low))
 
     d_mlp_gain = jnp.sum(dnormed_two * unit_two, axis=0)
     d_residual = grad_out + norm_back(dnormed_two * gain_two, unit_two, rstd_two)
@@ -471,38 +549,49 @@
         proj, total, d_mixed, lifted, reading, prior, later, through.reshape(1, kw), w_rank_out,
         bias, gate_low, dq, dk, dv, dg, seg_col, seg_row,
     )
-    dnormed_one = lax.psum(dot32(low_all, w_in, 1, 1).astype(low), "tensor").astype(f32)
+    dnormed_one = tensor_sum(dot32(low_all, w_in, 1, 1).astype(low))
     d_w_in = scatter(
         jnp.concatenate(
             [dot32(normed_one, low_all, 0, 0).astype(low), dot32(residual_low, gated, 0, 0).astype(low)],
             axis=1,
         )
     ).astype(f32)
+    mlp_part, dnormed_one = lax.optimization_barrier((mlp_part, dnormed_one))
+    dnormed_one = dnormed_one.astype(f32)
+    block_out = residual + tensor_sum(mlp_part).astype(f32)
     d_norm_gain = jnp.sum(dnormed_one * unit_one, axis=0)
     d_block_in = d_residual + norm_back(dnormed_one * gain_one, unit_one, rstd_one)
-    gains = scatter(jnp.stack([d_norm_gain, d_mlp_gain], axis=1))
-    d_rank_in = lax.psum(d_w_in[:, base : base + rank], "tensor")
+    index = lax.axis_index("dp") * peers + here
+    width_here = norm_gain.shape[0]
+    gains = lax.psum(jnp.stack([d_norm_gain, d_mlp_gain]), ("dp", "context"))
+    gains = lax.dynamic_slice_in_dim(gains, index * width_here, width_here, axis=1)
     small = lax.psum(
-        jnp.concatenate([rank_out_part.reshape(-1), bias_part[0]]), ("dp", "context")
-    )
-    d_group = lax.psum(gain_part[0], ("dp", "context", "tensor"))
+        jnp.concatenate([rank_out_part.reshape(-1), bias_part[0], gain_part[0]]),
+        ("dp", "context"),
+    )
+    d_rank_in = d_w_in[:, base : base + rank]
+    across = lax.psum(
+        jnp.concatenate([d_rank_in.reshape(-1), small[kw * (rank + 1) :]]), "tensor"
+    )
+    d_rank_in = across[: d_rank_in.size].reshape(d_rank_in.shape)
+    d_group = across[d_rank_in.size :]
     return (
         block_out[None],
         d_block_in[None],
-        gains[:, 0],
+        gains[0],
         d_w_in[:, :kw],
         d_w_in[:, kw : 2 * kw],
         d_w_in[:, 2 * kw : 2 * kw + vw],
         d_w_in[:, 2 * kw + vw : base],
         d_rank_in,
         small[: kw * rank].reshape(kw, rank),
-        small[kw * rank :],
+        small[kw * rank : kw * (rank + 1)],
         d_group,
         d_w_in[:, wide:],
-        gains[:, 1],
-        d_w_gate.astype(f32),
-        d_w_up.astype(f32),
-        d_w_down.astype(f32),
+        gains[1],
+        d_mlp[:, :hidden],
+        d_mlp[:, hidden : 2 * hidden],
+        d_mlp[:, 2 * hidden :],
     )
 
 

time: 627 us -> 369 us (0.59)
  waiting for transfers between devices: 355 us -> 30.6 us
  Pallas kernels: 22.7 us -> 135 us
  blocking collectives: 125 us -> 104 us
  matrix products: 41.7 us -> 27.2 us
  local copies, waits for them, and re-layouts: 37.4 us -> 29.8 us
    psum x3 -> x0, waiting for transfers between devices: 150 us -> none  [the longest x1 52.6 us: per_device(): lax.psum(dot32(activation, down_w, 1, 1).astype(low), 'tensor').astype(f32)]
    unnamed x17 -> x8, waiting for transfers between devices: 123 us -> 0.1 us
    pallas_call x0 -> x4, Pallas kernels: none -> 112 us  [tensor_sum(): pl.pallas_call(functools.partial(sum_kernel, n), out_shape=jax.ShapeDtype...]
    all_gather x4 -> x2, waiting for transfers between devices: 81.1 us -> 13.4 us  [gather(): return lax.all_gather(value, ('dp', 'context'), axis=0, tiled=True)]
    psum x3 -> x2, blocking collectives: 80.4 us -> 46.9 us  [the longest x1 31.8 us: per_device(): gains = lax.psum(jnp.stack([d_norm_gain, d_mlp_gain]), ('dp', 'context'))]
    reduce_scatter x0 -> x2, waiting for transfers between devices: none -> 17.1 us  [scatter(): value = lax.psum_scatter(value, axis, scatter_dimension=0, tiled=True)]
    dot_general x15, matrix products: 41.7 us -> 27.2 us  [dot32(): lax.dot_general(a, b, (((ca,), (cb,)), ((), ())), preferred_element_type=...]
    all_gather x1, blocking collectives: 17.9 us -> 30.4 us  [per_device(): lax.all_gather(jnp.concatenate([state_local.reshape(kw, HEAD_V), jnp.broa...]
  transfers between devices with their start and end apart: 12 -> 6, of which waited for: 11 -> 3; matrix products, arithmetic and copies ran while one was open for 10% -> 15% of each run, Pallas kernels for 0% -> 25%
where the time goes in v2:
time: 369 us; the launch traced here: 368 us
  Pallas kernels  135 us (37%)
  blocking collectives  104 us (28%)
  waiting for transfers between devices  30.6 us (8%)
  local copies, waits for them, and re-layouts  29.8 us (8%)
  matrix products  27.2 us (7%)
  other arithmetic  25.2 us (7%)
  between operations  15.3 us (4%)
    pallas_call x4, Pallas kernels, tensor_sum(): pl.pallas_call(functools.partial(sum_kernel, n), out_shape=jax.ShapeDtype...  112 us
    psum x1, blocking collectives, per_device(): gains = lax.psum(jnp.stack([d_norm_gain, d_mlp_gain]), ('dp', 'context'))  31.8 us
    all_gather x1, blocking collectives, per_device(): lax.all_gather(jnp.concatenate([state_local.reshape(kw, HEAD_V), jnp.broa...  30.4 us
    dot_general x15, matrix products, dot32(): lax.dot_general(a, b, (((ca,), (cb,)), ((), ())), preferred_element_type=...  27.2 us
    pallas_call x5, Pallas kernels, call(): pl.pallas_call(kernel, out_shape=[jax.ShapeDtypeStruct(shape, kind) for s...  22.7 us
    unnamed x61, local copies, waits for them, and re-layouts  20.2 us
    reduce_scatter x2, waiting for transfers between devices, scatter(): value = lax.psum_scatter(value, axis, scatter_dimension=0, tiled=True)  17.1 us
    psum x1, blocking collectives, per_device(): lax.psum(jnp.concatenate([d_rank_in.reshape(-1), small[kw * (rank + 1):]]...  15.2 us
  transfers between devices with their start and end apart: 6, of which 3 were waited for; matrix products, arithmetic and copies ran while one was open for 15% of the time, Pallas kernels for 25%

profile of v2, /device:TPU:0, one launch (start us, length us, event | category | flops | bytes accessed | tf_op | source)
XLA Modules:
  0.0 367.6 jit_solution(1708463966762024710)
XLA Ops:
  7.3 0.9 copy.80
  9.8 1.8 concatenate.38
  11.6 2.0 pad_maximum_fusion.2
  14.3 1.4 fusion.46
  15.6 12.7 %all-gather.2 = f32[4,1,2]{2,1,0:T(1,128)S(1)} all-gather(f32[1,1,2]{2,1,0:T(1,128)S(1)} %fusion.46), channel_id=1, replica_groups=mesh['dp'=2,'context'=4,'tensor'=4] {'context'}, dimensions={0}, use_global_device_ids=true | all-gather | bytes 40 | tf_op jit(solution)/shard_map/all_gather | solution.py:460
  32.5 13.4 %all-gather.6.cloned.1.call-done = bf16[1024,1152]{1,0:T(8,128)(2,1)} async-done(((bf16[128,1152]{1,0:T(8,128)(2,1)}), bf16[1024,1152]{1,0:T(8,128)(2,1)}) %all-gather.6.cloned.1.call-update) | async-done | bytes 2359312 | tf_op jit(solution)/shard_map/all_gather | solution.py:392
  45.9 1.4 convert_reduce_fusion
  47.3 4.0 %fusion.16.proj = f32[512,896]{1,0:T(8,128)} fusion(bf16[1024,1152]{1,0:T(8,128)(2,1)} %all-gather.6.cloned.1.call-done, f32[1,512,1024]{2,1,0:T(8,128)S(1)} %copy-done.1, f32[1024]{0:T(1024)S(1)} %get-tuple-element.125, f32[512]{0:T(512)S(1)} %add_rsqrt_fusion.1), kind=kOutput, calls=%fused_computation.35 | convolution fusion | flops 941096960 | bytes 5773312 | tf_op jit(solution)/shard_map/dot_general | solution.py:402
  51.3 5.6 %shard_map.288 = (f32[512,256]{1,0:T(8,128)}, f32[1,128,256]{2,1,0:T(8,128)}, bf16[512,128]{1,0:T(8,128)(2,1)}, f32[512,128]{1,0:T(8,128)}, f32[1,128]{1,0:T(1,128)}) custom-call(f32[512,896]{1,0:T(8,128)} %fusion.16.proj, f32[128,16]{1,0:T(8,128)} %copy.83.rank_out, f32[1,128]{1,0:T(1,128)} %bitcast.164, s32[512,1]{1,0:T(8,128)} %copy.84.seg_col, ...), custom_call_target="tpu_custom_call" | custom-call | tf_op jit(solution)/shard_map/pallas_call | solution.py:308
  57.7 0.9 pad_maximum_fusion.3
  58.6 30.4 %all-gather = f32[512,384]{1,0:T(8,128)S(1)} all-gather(f32[128,384]{1,0:T(8,128)S(1)} %pad_maximum_fusion.3), channel_id=2, replica_groups=mesh['dp'=2,'context'=4,'tensor'=4] {'context'}, dimensions={0}, use_global_device_ids=true | all-gather | bytes 983040 | tf_op jit(solution)/shard_map/all_gather | solution.py:461
  90.2 2.9 shard_map.289
  93.1 1.7 convolution_convert_fusion.5.x_ref
  94.9 27.2 %shard_map.290 = bf16[512,1024]{1,0:T(8,128)(2,1)S(1)} custom-call(bf16[512,1024]{1,0:T(8,128)(2,1)S(1)} %convolution_convert_fusion.5.x_ref), custom_call_target="tpu_custom_call" | custom-call | tf_op jit(solution)/shard_map/pallas_call | solution.py:366
  122.4 1.4 multiply_convert_fusion
  123.9 2.8 fusion.29
  127.2 0.9 fusion.25
  128.7 2.4 multiply_convert_fusion.2
  131.1 1.0 fusion.27
  132.2 1.0 add_convert_fusion.x_ref
  133.3 27.2 %shard_map.291 = bf16[512,1024]{1,0:T(8,128)(2,1)S(1)} custom-call(bf16[512,1024]{1,0:T(8,128)(2,1)S(1)} %add_convert_fusion.x_ref), custom_call_target="tpu_custom_call" | custom-call | tf_op jit(solution)/shard_map/pallas_call | solution.py:366
  162.7 1.9 copy-done.9
  164.6 1.3 fusion.32.d_gated_in
  165.9 3.2 shard_map.292
  169.1 0.9 convert_element_type.144
  170.0 14.1 %all-gather.1 = bf16[4,128,256]{2,1,0:T(8,128)(2,1)S(1)} all-gather(bf16[1,128,256]{2,1,0:T(8,128)(2,1)S(1)} %convert_element_type.144), channel_id=3, replica_groups=mesh['dp'=2,'context'=4,'tensor'=4] {'context'}, dimensions={0}, use_global_device_ids=true | all-gather | bytes 327680 | tf_op jit(solution)/shard_map/all_gather | solution.py:532
  185.6 6.0 %shard_map.293 = (f32[512,128]{1,0:T(8,128)}, f32[512,128]{1,0:T(8,128)}, f32[512,256]{1,0:T(8,128)}, f32[512,128]{1,0:T(8,128)}) custom-call(f32[512,896]{1,0:T(8,128)} %fusion.16.proj, f32[512,128]{1,0:T(8,128)} %get-tuple-element.41.total_in, bf16[512,256]{1,0:T(8,128)(2,1)} %get-tuple-element.43.d_mixed, s32[512,1]{1,0:T(8,128)} %copy.84.seg_col, ...), custom_call_target="tpu_custom_call" | custom-call | tf_op jit(solution)/shard_map/pallas_call | solution.py:308
  191.5 5.1 %shard_map.294 = (bf16[512,896]{1,0:T(8,128)(2,1)}, f32[128,16]{1,0:T(8,128)}, f32[1,128]{1,0:T(1,128)}) custom-call(f32[512,896]{1,0:T(8,128)} %fusion.16.proj, f32[512,128]{1,0:T(8,128)} %get-tuple-element.41.total_in, bf16[512,256]{1,0:T(8,128)(2,1)} %get-tuple-element.43.d_mixed, bf16[512,128]{1,0:T(8,128)(2,1)} %get-tuple-element.37.lifted, ...), custom_call_target="tpu_custom_call" | custom-call | tf_op jit(solution)/shard_map/pallas_call | solution.py:308
  196.6 2.4 convolution_convert_fusion
  199.0 1.6 pad_maximum_fusion.1
  200.7 2.5 convolution_convert_fusion.1
  205.9 2.4 pad_maximum_fusion
  208.4 4.3 %reduce-scatter.9.cloned.1.call-done = bf16[512,1152]{0,1:T(8,128)(2,1)} async-done(((bf16[1024,1152]{0,1:T(8,128)(2,1)}), bf16[512,1152]{0,1:T(8,128)(2,1)}) %reduce-scatter.9.cloned.1.call-update) | async-done | bytes 1179664 | tf_op jit(solution)/shard_map/reduce_scatter | solution.py:397
  212.7 2.4 copy.99
  215.4 12.8 %reduce-scatter.11.cloned.1.call-done = bf16[512,2112]{0,1:T(8,128)(2,1)} async-done(((bf16[1024,2112]{0,1:T(8,128)(2,1)}), bf16[512,2112]{0,1:T(8,128)(2,1)}) %reduce-scatter.11.cloned.1.call-update) | async-done | bytes 2162704 | tf_op jit(solution)/shard_map/reduce_scatter | solution.py:397
  228.2 4.1 %copy.101 = bf16[512,2112]{1,0:T(8,128)(2,1)} copy(bf16[512,2112]{0,1:T(8,128)(2,1)} %reduce-scatter.11.cloned.1.call-done) | data formatting | bytes 4325376
  232.4 2.5 fusion.18.x_ref
  234.8 29.2 %shard_map.295 = bf16[512,1024]{1,0:T(8,128)(2,1)S(1)} custom-call(bf16[512,1024]{1,0:T(8,128)(2,1)S(1)} %fusion.18.x_ref), custom_call_target="tpu_custom_call" | custom-call | tf_op jit(solution)/shard_map/pallas_call | solution.py:366
  264.1 2.4 convolution_convert_fusion.4.x_ref
  266.6 2.6 fusion.12
  269.2 31.8 %all-reduce = (f32[2,1024]{1,0:T(2,128)S(1)}, f32[2432]{0:T(1024)S(1)}) all-reduce(f32[2,1024]{1,0:T(2,128)S(1)} %pad_maximum_fusion.6, f32[2432]{0:T(1024)S(1)} %pad_maximum_fusion.4), channel_id=1, replica_groups=mesh['dp'=2,'context'=4,'tensor'=4] {'dp','context'}, use_global_device_ids=true, to_apply=%region_7.8 | all-reduce | flops 4480 | bytes 35840 | tf_op jit(solution)/shard_map/psum | solution.py:566
  301.5 28.6 %shard_map.296 = bf16[512,1024]{1,0:T(8,128)(2,1)S(1)} custom-call(bf16[512,1024]{1,0:T(8,128)(2,1)S(1)} %convolution_convert_fusion.4.x_ref), custom_call_target="tpu_custom_call" | custom-call | tf_op jit(solution)/shard_map/pallas_call | solution.py:366
  331.4 3.5 add_bitcast_fusion
  334.9 1.9 fusion.7
  336.8 1.2 copy.100
  338.1 15.2 %psum.23 = f32[2304]{0:T(1024)S(1)} all-reduce(f32[2304]{0:T(1024)S(1)} %pad_maximum_fusion.5), channel_id=1, replica_groups=mesh['dp'=2,'context'=4,'tensor'=4] {'tensor'}, use_global_device_ids=true, to_apply=%region_11.12 | all-reduce | flops 2304 | bytes 18432 | tf_op jit(solution)/shard_map/psum | solution.py:573
  358.4 1.3 copy.102
  359.8 1.0 fusion.51
  (125 shorter events, 23.3 us)
Async XLA Ops:
  7.2 6.5 %copy-start.16 = (s32[1,512]{1,0:T(1,128)S(1)}, s32[1,512]{1,0:T(1,128)}, u32[]{:S(2)}) copy-start(s32[1,512]{1,0:T(1,128)} %seg_row.5) | copy-start | bytes 6148
  7.2 21.2 %copy-start.17 = (f32[128,16]{0,1:T(8,128)S(1)}, f32[128,16]{0,1:T(8,128)}, u32[]{:S(2)}) copy-start(f32[128,16]{0,1:T(8,128)} %param.26) | copy-start | bytes 24580
  7.2 25.1 %copy-start.1 = (f32[1,512,1024]{2,1,0:T(8,128)S(1)}, f32[1,512,1024]{2,1,0:T(8,128)}, u32[]{:S(2)}) copy-start(f32[1,512,1024]{2,1,0:T(8,128)} %param.17) | copy-start | bytes 6291460
  7.2 38.7 %all-gather.6.cloned.1.call-start = ((), (), s32[]{:S(2)}) async-start(), calls=%async_computation.4 | async-start | bytes 2654208 | tf_op jit(solution)/shard_map/all_gather | solution.py:392
  11.6 112.3 %all-gather.8.cloned.1.call-start = ((), (), s32[]{:S(2)}) async-start(), calls=%async_computation.5 | async-start | bytes 4866048 | tf_op jit(solution)/shard_map/all_gather | solution.py:392
  13.6 199.1 %reduce-scatter.9.cloned.1.call-start = ((), (), s32[]{:S(2)}) async-start(), calls=%async_computation.6 | async-start | bytes 3538944 | tf_op jit(solution)/shard_map/reduce_scatter | solution.py:397
  93.1 28.9 %copy-start.2 = (f32[1,512,1024]{2,1,0:T(8,128)S(1)}, f32[1,512,1024]{2,1,0:T(8,128)}, u32[]{:S(2)}) copy-start(f32[1,512,1024]{2,1,0:T(8,128)} %param.17) | copy-start | bytes 6291460
  122.4 38.8 %copy-start = (f32[512,1024]{1,0:T(8,128)}, f32[512,1024]{1,0:T(8,128)S(1)}, u32[]{:S(2)}) copy-start(f32[512,1024]{1,0:T(8,128)S(1)} %get-tuple-element.135) | copy-start | bytes 6291460
  123.9 2.8 copy-start.10
  123.9 3.3 copy-start.20
  127.2 1.6 copy-start.7
  131.1 1.0 copy-start.22
  131.1 1.1 copy-start.21
  161.2 1.0 copy-start.12
  162.2 3.7 %copy-start.5 = (f32[512,1024]{1,0:T(8,128)}, f32[512,1024]{1,0:T(8,128)S(1)}, u32[]{:S(2)}) copy-start(f32[512,1024]{1,0:T(8,128)S(1)} %fusion.10) | copy-start | bytes 6291460
  162.2 2.4 copy-start.9
  191.5 5.1 %copy-start.3 = (f32[1,512,1024]{2,1,0:T(8,128)S(1)}, f32[1,512,1024]{2,1,0:T(8,128)}, u32[]{:S(2)}) copy-start(f32[1,512,1024]{2,1,0:T(8,128)} %param.17) | copy-start | bytes 6291460
  200.7 27.5 %reduce-scatter.11.cloned.1.call-start = ((), (), s32[]{:S(2)}) async-start(), calls=%async_computation.7 | async-start | bytes 6488064 | tf_op jit(solution)/shard_map/reduce_scatter | solution.py:397
  200.7 2.5 copy-start.11
  200.7 2.5 copy-start.23
  203.2 1.6 copy-start.8
  203.3 1.7 copy-start.13
  208.3 128.4 %reduce-scatter.13.cloned.1.call-start = ((), (), s32[]{:S(2)}) async-start(), calls=%async_computation.8 | async-start | bytes 1474560
  215.1 143.3 %reduce-scatter.15.cloned.1.call-start = ((), (), s32[]{:S(2)}) async-start(), calls=%async_computation.9 | async-start | bytes 2785280
  234.8 29.2 %copy-start.14 = (bf16[512,704]{0,1:T(8,128)(2,1)S(1)}, bf16[512,704]{0,1:T(8,128)(2,1)}, u32[]{:S(2)}) copy-start(bf16[512,704]{0,1:T(8,128)(2,1)} %get-tuple-element.140) | copy-start | bytes 2162692
  264.1 2.4 copy-start.15
  266.5 2.7 copy-start.18
  266.5 2.7 copy-start.19
  331.4 3.5 copy-start.4
  331.4 3.5 copy-start.6
Sparse Core Ops, SparseCore 0:
  11.7 34.1 all-gather.5
  47.5 60.7 all-gather.7
  200.8 11.8 reduce-scatter.8
  214.9 13.2 reduce-scatter.10
  230.4 30.5 reduce-scatter.12
  263.2 45.4 reduce-scatter.14
